TPU v7x, 256 devices: a whole 4x4x8 slice. The times are simulated.
256 devices in a mesh: gx: 32 (over y, z), gy: 8 (over x, core).
Axes of the slice: x: 4, y: 4, z: 8, core: 2. Of those that a mesh axis runs over, the one named last changes fastest.
Arguments:
- offsets: float32 [3, 64, 16, 1024], P(None, 'gx', 'gy'), as said below
- charges: float32 [64, 16, 1024], P('gx', 'gy'), may hold values from -0.08 to 0.08
Outputs:
- potential: float32 [64, 16, 1024], P('gx', 'gy')
Inputs may be any that keep to these rules, and one draw needn't show every extreme that they name: `offsets`: particle p of a leaf lies in sub-cell (p // 4^2, (p // 4) % 4, p % 4) of the leaf's grid of 4^3 equal sub-cells, inside the middle half of that sub-cell along each dimension.
All inputs are finite; a program needn't handle non-finite values. Where the computation divides by a largest or mean magnitude, that divisor is 1e-20 or more.
Results may differ from a plain program's by a relative error of at most 0.0003.
Values sent between devices are 32-bit elements; how exact they have to be, the bound alone decides.
A program may use at most 192 MiB of HBM per device.

v0:
```python
import jax
import jax.numpy as jnp
from jax import lax
from jax.sharding import PartitionSpec as P

CX = 2
CY = 2
LZ = 16
PPL = 64


highest = lax.Precision.HIGHEST


def padded_2(block, sides, width):
    for axis, dim in sides:
        count = lax.axis_size(axis)
        forward = [(i, i + 1) for i in range(count - 1)]
        backward = [(target, source) for source, target in forward]
        low = lax.ppermute(
            lax.slice_in_dim(block, block.shape[dim] - width, None, axis=dim), axis, forward
        )
        high = lax.ppermute(lax.slice_in_dim(block, 0, width, axis=dim), axis, backward)
        block = jnp.concatenate([low, block, high], axis=dim)
    return block


def cheb_points():
    return jnp.cos((2.0 * jnp.arange(4, dtype=jnp.float32) + 1.0) * jnp.pi / 8.0)


def interpolate(coords):
    points = cheb_points()
    second = 2.0 * points * points - 1.0
    third = 4.0 * points * points * points - 3.0 * points
    value = coords[..., None]
    return 0.25 + 0.5 * (
        value * points
        + (2.0 * value * value - 1.0) * second
        + (4.0 * value * value * value - 3.0 * value) * third
    )


def node_grid():
    points = cheb_points()
    counter = jnp.arange(64, dtype=jnp.int32)
    return jnp.stack([points[counter // 16], points[counter // 4 % 4], points[counter % 4]], -1)


def child_grid():
    counter = jnp.arange(8, dtype=jnp.int32)
    return jnp.stack([counter // 4, counter // 2 % 2, counter % 2], -1).astype(jnp.float32)


def upward_matrix():
    points = cheb_points()
    halves = jnp.array([0.0, 1.0], dtype=jnp.float32)
    shifted = (points[None, :] + 2.0 * halves[:, None] - 1.0) / 2.0
    factor = interpolate(shifted)
    return jnp.einsum("xia,yjb,zkc->xyzijkabc", factor, factor, factor, precision=highest).reshape(
        512, 64
    )


def translation(offset):
    node_points = node_grid()
    child_corner = child_grid()
    box_offsets = 2.0 * offset[None, None, :] + child_corner[:, None, :] - child_corner[None, :, :]
    spread = (node_points[None, :, :] - node_points[:, None, :]) / 2.0
    separation = spread[None, :, None, :, :] - box_offsets[:, None, :, None, :]
    adjacent = (jnp.max(jnp.abs(box_offsets), -1) <= 1.0).astype(jnp.float32)[:, None, :, None]
    distance = jnp.sqrt(jnp.sum(separation * separation, -1))
    return ((1.0 - adjacent) / (distance + adjacent)).reshape(512, 512)


def offset_of(counter):
    return jnp.stack([counter // 9, counter // 3 % 3, counter % 3]) - 1


def translation_tables():

    def one_table(counter):
        return translation(offset_of(counter).astype(jnp.float32))

    return lax.map(one_table, jnp.arange(27, dtype=jnp.int32))


def to_parent(moments):
    size_x, size_y, size_z, _ = moments.shape
    moments = moments.reshape(size_x // 2, 2, size_y // 2, 2, size_z // 2, 2, 64)
    return moments.transpose(0, 2, 4, 1, 3, 5, 6).reshape(
        size_x // 2, size_y // 2, size_z // 2, 512
    )


def from_parent(moments):
    size_x, size_y, size_z, _ = moments.shape
    moments = moments.reshape(size_x, size_y, size_z, 2, 2, 2, 64)
    return moments.transpose(0, 3, 1, 4, 2, 5, 6).reshape(2 * size_x, 2 * size_y, 2 * size_z, 64)


def matmul(left, right):
    return jnp.dot(left, right, precision=highest, preferred_element_type=jnp.float32)


def coarsen(moments, upward):
    parents = to_parent(moments)
    return matmul(parents.reshape(-1, 512), upward).reshape(parents.shape[:3] + (64,))


def refine(local, upward):
    spread_out = matmul(local.reshape(-1, 64), upward.T).reshape(local.shape[:3] + (512,))
    return from_parent(spread_out)


def pad_one(moments):
    return jnp.pad(moments, ((1, 1), (1, 1), (1, 1), (0, 0)))


def far_translate(padded, scaling, tables):
    size_x, size_y, size_z = (padded.shape[0] - 2, padded.shape[1] - 2, padded.shape[2] - 2)

    def step_fn(running, inputs):
        counter, table = inputs
        offset = offset_of(counter)
        window_piece = lax.dynamic_slice(
            padded,
            (offset[0] + 1, offset[1] + 1, offset[2] + 1, jnp.int32(0)),
            (size_x, size_y, size_z, 512),
        )
        return (running + matmul(window_piece.reshape(-1, 512), table), None)

    running, _ = lax.scan(
        step_fn,
        jnp.zeros((size_x * size_y * size_z, 512), jnp.float32),
        (jnp.arange(27, dtype=jnp.int32), tables),
    )
    return (scaling * running).reshape(size_x, size_y, size_z, 512)


def dense_translate(targets, sources, weights):
    node_points = node_grid()
    spread = (node_points[:, None, :] - node_points[None, :, :]) / 2.0
    box_offsets = sources[None, :, :] - targets[:, None, :]
    separation = spread[None, :, None, :, :] - box_offsets[:, None, :, None, :]
    adjacent = (jnp.max(jnp.abs(box_offsets), -1) <= 1.0).astype(jnp.float32)[:, None, :, None]
    distance = jnp.sqrt(jnp.sum(separation * separation, -1))
    kernel = ((1.0 - adjacent) / (distance + adjacent)).reshape(
        targets.shape[0] * 64, sources.shape[0] * 64
    )
    return (0.125 * matmul(kernel, weights.reshape(-1))).reshape(targets.shape[0], 64)


def particle_basis(offsets):
    coords = 2.0 * offsets - 1.0
    along_x = interpolate(coords[0])
    along_y = interpolate(coords[1])
    along_z = interpolate(coords[2])
    product = (
        along_x[..., :, None, None] * along_y[..., None, :, None] * along_z[..., None, None, :]
    )
    return product.reshape(along_x.shape[:-1] + (64,))


def gather_moments(charges, interp_basis):
    return jnp.einsum(
        "...p,...pm->...m",
        charges,
        interp_basis,
        precision=highest,
        preferred_element_type=jnp.float32,
    )


def evaluate_local(interp_basis, local):
    return jnp.einsum(
        "...pm,...m->...p",
        interp_basis,
        local,
        precision=highest,
        preferred_element_type=jnp.float32,
    )


def near_field(targets, sources, weights):
    size_x, size_y, depth, count = (
        targets.shape[1],
        targets.shape[2],
        targets.shape[3],
        targets.shape[4],
    )
    self_mask = jnp.concatenate(
        [
            jnp.zeros((count, count), jnp.float32),
            jnp.eye(count, dtype=jnp.float32),
            jnp.zeros((count, count), jnp.float32),
        ],
        1,
    )
    running = jnp.zeros((size_x, size_y, depth, count), jnp.float32)
    for step_x in range(3):
        for step_y in range(3):
            window = sources[:, step_x : step_x + size_x, step_y : step_y + size_y]
            stacked = jnp.concatenate(
                [
                    window[..., 0:depth, :],
                    window[..., 1 : depth + 1, :],
                    window[..., 2 : depth + 2, :],
                ],
                -1,
            )
            charge_win = weights[step_x : step_x + size_x, step_y : step_y + size_y]
            charge_win = jnp.concatenate(
                [
                    charge_win[..., 0:depth, :],
                    charge_win[..., 1 : depth + 1, :],
                    charge_win[..., 2 : depth + 2, :],
                ],
                -1,
            )
            squared = jnp.zeros((size_x, size_y, depth, count, 3 * count), jnp.float32)
            for comp in range(3):
                differ = targets[comp][..., :, None] - stacked[comp][..., None, :]
                squared = squared + differ * differ
            if step_x == 1 and step_y == 1:
                inverse = lax.rsqrt(squared + self_mask) * (1.0 - self_mask)
            else:
                inverse = lax.rsqrt(squared)
            running = running + jnp.sum(inverse * charge_win[..., None, :], -1)
    return running


def body(offsets, charges):
    index_x = lax.axis_index("gx")
    index_y = lax.axis_index("gy")
    count_x = lax.axis_size("gx")
    count_y = lax.axis_size("gy")
    upward = upward_matrix()
    tables = translation_tables()
    stacked = jnp.concatenate([offsets, charges[None]], 0)
    own_basis = particle_basis(offsets.reshape(3, CX, CY, LZ, PPL))
    own_charges = charges.reshape(CX, CY, LZ, PPL)
    leaf_moments = gather_moments(own_charges, own_basis)
    rim_flat = padded_2(leaf_moments.reshape(CX, CY, LZ * 64), (("gx", 0), ("gy", 1)), 2)
    rim_moments = rim_flat.reshape(CX + 4, CY + 4, LZ, 64)
    near_block = padded_2(stacked, (("gx", 1), ("gy", 2)), 1).reshape(4, CX + 2, CY + 2, LZ, PPL)
    rim_padded = jnp.pad(rim_moments, ((0, 0), (0, 0), (2, 2), (0, 0)))
    leaf_far = from_parent(far_translate(to_parent(rim_padded), 1.0, tables))
    first_moments = coarsen(leaf_moments, upward)
    first_piece = first_moments.reshape(1, CY // 2, LZ // 2 * 64)
    gathered = lax.all_gather(first_piece, ("gx", "gy"), axis=0, tiled=True)
    first_whole = gathered.reshape(count_x, count_y * (CY // 2), LZ // 2, 64)
    second_whole = coarsen(first_whole, upward)
    first_block = lax.dynamic_slice(
        pad_one(to_parent(first_whole)),
        (index_x // 2, index_y // 2, 0, 0),
        (3, 3, LZ // 4 + 2, 512),
    )
    third_whole = coarsen(second_whole, upward)
    first_far = from_parent(far_translate(first_block, 0.5, tables))
    first_far = lax.dynamic_slice(first_far, (index_x % 2, index_y % 2, 0, 0), (1, 1, LZ // 2, 64))
    second_block = lax.dynamic_slice(
        pad_one(to_parent(second_whole)),
        (index_x // 4, index_y // 4, 0, 0),
        (3, 3, LZ // 8 + 2, 512),
    )
    second_far = from_parent(far_translate(second_block, 0.25, tables))
    second_far = lax.dynamic_slice(
        second_far, (index_x // 2 % 2, index_y // 2 % 2, 0, 0), (1, 1, LZ // 4, 64)
    )
    boxes_x, boxes_y, boxes_z = (count_x * CX // 8, count_y * CY // 8, LZ // 8)
    counter = jnp.arange(boxes_x * boxes_y * boxes_z, dtype=jnp.int32)
    sources = jnp.stack(
        [counter // (boxes_y * boxes_z), counter // boxes_z % boxes_y, counter % boxes_z], -1
    ).astype(jnp.float32)
    targets = jnp.stack(
        [
            jnp.full((boxes_z,), index_x // 4, jnp.int32),
            jnp.full((boxes_z,), index_y // 4, jnp.int32),
            jnp.arange(boxes_z, dtype=jnp.int32),
        ],
        -1,
    ).astype(jnp.float32)
    top_far = dense_translate(targets, sources, third_whole.reshape(-1, 64))
    second_local = refine(top_far.reshape(1, 1, boxes_z, 64), upward)
    second_local = (
        lax.dynamic_slice(
            second_local, (index_x // 2 % 2, index_y // 2 % 2, 0, 0), (1, 1, LZ // 4, 64)
        )
        + second_far
    )
    first_local = refine(second_local, upward)
    first_local = (
        lax.dynamic_slice(first_local, (index_x % 2, index_y % 2, 0, 0), (1, 1, LZ // 2, 64))
        + first_far
    )
    leaf_local = refine(first_local, upward) + leaf_far
    far_potential = evaluate_local(own_basis, leaf_local)
    padded = jnp.pad(near_block, ((0, 0), (0, 0), (0, 0), (1, 1), (0, 0)))
    grid_x = (index_x * CX - 1 + jnp.arange(CX + 2, dtype=jnp.int32)).astype(jnp.float32)
    grid_y = (index_y * CY - 1 + jnp.arange(CY + 2, dtype=jnp.int32)).astype(jnp.float32)
    grid_z = jnp.arange(-1, LZ + 1, dtype=jnp.int32).astype(jnp.float32)
    positions = jnp.stack(
        [
            padded[0] + grid_x[:, None, None, None],
            padded[1] + grid_y[None, :, None, None],
            padded[2] + grid_z[None, None, :, None],
        ]
    )
    near_potential = near_field(positions[:, 1:-1, 1:-1, 1:-1], positions, padded[3])
    return (far_potential + near_potential).reshape(CX, CY, LZ * PPL)


def solution(mesh):
    in_specs = (P(None, "gx", "gy", None), P("gx", "gy", None))
    out_specs = P("gx", "gy", None)
    return jax.shard_map(body, mesh=mesh, in_specs=in_specs, out_specs=out_specs, check_vma=False)
```

profile of v0, /device:TPU:1, one launch (start us, length us, event | category | flops | bytes accessed | tf_op | source)
XLA Modules:
  0.0 1349.1 jit_solution(7207719074054783453)
XLA Ops:
  9.9 5.6 collective-permute-start
  16.2 3.6 collective-permute-start.4
  22.0 2.4 compare_select_fusion.29
  24.4 2.4 compare_select_fusion.23
  27.7 2.6 multiply_bitcast_fusion
  30.2 6.6 dot_general.84
  36.9 6.0 reshape.1491
  43.3 75.7 %all_gather.3 = f32[256,1,512]{2,1,0:T(1,128)S(1)} all-gather(f32[1,1,512]{2,1,0:T(1,128)S(1)} %reshape_reshape.29), channel_id=1, replica_groups=mesh['gx'=32,'gy'=8] {'gx','gy'}, dimensions={0}, use_global_device_ids=true | all-gather | bytes 526336 | tf_op jit(solution)/shard_map/all_gather | solution.py:251
  129.6 2.9 reshape.1306
  137.7 354.1 %while.55 = (s32[]{:T(128)}, f32[27,512,512]{2,1,0:T(8,128)}, s32[27]{0:T(128)S(1)}, s32[]{:T(128)}, s32[1]{0:T(128)}, /*index=5*/s32[]{:T(128)}, s32[]{:T(128)}...) while((s32[]{:T(128)}, f32[27,512,512]{2,1,0:T(8,128)}, s32[27]{0:T(128)S(1)}, s32[]{:T(128)}, ...), condition=%wide.region_5.6_spmd, body=%wide.region_2.5_spmd.sunk | while | flops 2651413 | bytes 7449731 | solution.py:85
  144.9 2.3 compare_select_fusion.34
  158.0 2.3 compare_select_fusion.34
  171.1 2.3 compare_select_fusion.34
  184.2 2.3 compare_select_fusion.34
  197.2 2.3 compare_select_fusion.34
  492.7 263.9 %while.57 = (s32[]{:T(128)}, f32[4,512]{1,0:T(4,128)S(1)}, s32[27]{0:T(128)S(1)}, f32[3,3,6,512]{3,0,2,1:T(4,128)S(1)}, f32[27,512,512]{2,1,0:T(8,128)}, /*index...) while((s32[]{:T(128)}, f32[4,512]{1,0:T(4,128)S(1)}, ...), condition=%wide.region_9.10_spmd.clone, body=%wide.region_8.9_spmd.clone.sunk | while | flops 12587056 | bytes 1090143 | solution.py:133
  756.7 263.8 %while.56 = (s32[]{:T(128)}, f32[2,512]{1,0:T(2,128)S(1)}, s32[27]{0:T(128)S(1)}, f32[3,3,4,512]{3,0,2,1:T(4,128)S(1)}, f32[27,512,512]{2,1,0:T(8,128)}, /*index...) while((s32[]{:T(128)}, f32[2,512]{1,0:T(2,128)S(1)}, ...), condition=%wide.region_7.8_spmd.clone, body=%wide.region_6.7_spmd.clone.sunk | while | flops 6293552 | bytes 1069663 | solution.py:133
  1027.7 3.5 collective-permute-start.2
  1034.7 3.0 collective-permute-start.7
  1038.7 280.9 %while.58 = (s32[]{:T(128)}, f32[8,512]{1,0:T(8,128)S(1)}, s32[27]{0:T(128)S(1)}, f32[3,3,10,512]{3,2,1,0:T(8,128)S(1)}, f32[27,512,512]{2,1,0:T(8,128)}, /*inde...) while((s32[]{:T(128)}, f32[8,512]{1,0:T(8,128)S(1)}, ...), condition=%wide.region_11.12_spmd.clone, body=%wide.region_10.11_spmd.clone.sunk | while | flops 25174064 | bytes 1098335 | solution.py:133
  1321.1 3.3 fusion.63
  1328.0 4.6 multiply_reduce_fusion.3
  1332.6 7.4 multiply_reduce_fusion.10
  1340.0 8.3 multiply_reduce_fusion.9
  (1097 shorter events, 556.4 us)
Async XLA Ops:
  2.3 13.2 copy-start.3
  2.3 13.2 copy-start.4
  6.0 30.9 %copy-start = (f32[2,2,16,64,64]{4,3,2,1,0:T(8,128)}, f32[2,2,16,64,64]{4,3,2,1,0:T(8,128)S(1)}, u32[]{:S(2)}) copy-start(f32[2,2,16,64,64]{4,3,2,1,0:T(8,128)S(1)} %copy.105) | copy-start | bytes 3145732
  8.6 1016.3 %collective-permute-start.1 = (f32[2,2,1024]{2,1,0:T(2,128)}, f32[2,2,1024]{2,1,0:T(2,128)}, u32[]{:S(2)}, u32[]{:S(2)}) collective-permute-start(f32[2,2,1024]{2,1,0:T(2,128)} %reshape.1309), channel_id=1, source_target_pairs={{8,0},{16,8},{24,16},{32,24},{40,32},{48,40},{56,48},{64,56},{72,6... | collective-permute-start | bytes 49160 | tf_op jit(solution)/shard_map/ppermute | solution.py:23
  9.9 1013.5 %collective-permute-start = (f32[2,2,1024]{2,1,0:T(2,128)}, f32[2,2,1024]{2,1,0:T(2,128)}, u32[]{:S(2)}, u32[]{:S(2)}) collective-permute-start(f32[2,2,1024]{2,1,0:T(2,128)} %reshape.1309), channel_id=1, source_target_pairs={{0,8},{8,16},{16,24},{24,32},{32,40},{40,48},{48,56},{56,64},{64,7... | collective-permute-start | bytes 49160 | tf_op jit(solution)/shard_map/ppermute | solution.py:20
  16.2 1015.0 %collective-permute-start.4 = (f32[4,1,2,1024]{3,2,1,0:T(2,128)}, f32[4,1,2,1024]{3,2,1,0:T(2,128)}, u32[]{:S(2)}, u32[]{:S(2)}) collective-permute-start(f32[4,1,2,1024]{3,2,1,0:T(2,128)} %get-tuple-element.678), channel_id=1, source_target_pairs={{0,8},{8,16},{16,24},{24,32},{32,40},{40,48},{48,56},{56,64},{64,7... | collective-permute-start | bytes 98312 | tf_op jit(solution)/shard_map/ppermute | solution.py:20
  19.7 1011.5 %collective-permute-start.5 = (f32[4,1,2,1024]{3,2,1,0:T(2,128)}, f32[4,1,2,1024]{3,2,1,0:T(2,128)}, u32[]{:S(2)}, u32[]{:S(2)}) collective-permute-start(f32[4,1,2,1024]{3,2,1,0:T(2,128)} %get-tuple-element.679), channel_id=1, source_target_pairs={{8,0},{16,8},{24,16},{32,24},{40,32},{48,40},{56,48},{64,56},{72,6... | collective-permute-start | bytes 98312 | tf_op jit(solution)/shard_map/ppermute | solution.py:23
  756.7 264.0 %copy-start.5 = (f32[64,64]{1,0:T(8,128)S(1)}, f32[64,64]{1,0:T(8,128)}, u32[]{:S(2)}) copy-start(f32[64,64]{1,0:T(8,128)} %fusion.31) | copy-start | bytes 49156
  756.7 264.7 %copy-start.2 = (f32[2,2,2,64,64]{4,3,2,1,0:T(8,128)S(1)}, f32[2,2,2,64,64]{4,3,2,1,0:T(8,128)}, u32[]{:S(2)}) copy-start(f32[2,2,2,64,64]{4,3,2,1,0:T(8,128)} %dot_general.84) | copy-start | bytes 393220
  1025.6 12.1 collective-permute-start.3
  1027.7 10.1 collective-permute-start.2
  1032.8 291.7 %collective-permute-start.6 = (f32[4,4,1,1024]{3,2,1,0:T(1,128)}, f32[4,4,1,1024]{3,2,1,0:T(1,128)}, u32[]{:S(2)}, u32[]{:S(2)}) collective-permute-start(f32[4,4,1,1024]{3,2,1,0:T(1,128)} %get-tuple-element.674), channel_id=1, source_target_pairs={{0,1},{1,2},{2,3},{3,4},{4,5},{5,6},{6,7},{8,9},{9,10},{10,11},{11... | collective-permute-start | bytes 196616 | tf_op jit(solution)/shard_map/ppermute | solution.py:20
  1034.7 289.8 %collective-permute-start.7 = (f32[4,4,1,1024]{3,2,1,0:T(1,128)}, f32[4,4,1,1024]{3,2,1,0:T(1,128)}, u32[]{:S(2)}, u32[]{:S(2)}) collective-permute-start(f32[4,4,1,1024]{3,2,1,0:T(1,128)} %get-tuple-element.675), channel_id=1, source_target_pairs={{1,0},{2,1},{3,2},{4,3},{5,4},{6,5},{7,6},{9,8},{10,9},{11,10},{12... | collective-permute-start | bytes 196616 | tf_op jit(solution)/shard_map/ppermute | solution.py:23
  1038.2 282.9 %copy-start.1 = (f32[2,2,16,64,64]{4,3,2,1,0:T(8,128)S(1)}, f32[2,2,16,64,64]{4,3,2,1,0:T(8,128)}, u32[]{:S(2)}) copy-start(f32[2,2,16,64,64]{4,3,2,1,0:T(8,128)} %copy-done) | copy-start | bytes 3145732
  1038.7 287.2 %copy-start.8 = (f32[4]{0:T(128)S(1)}, f32[4]{0:T(128)}, u32[]{:S(2)}) copy-start(f32[4]{0:T(128)} %add_convert_fusion.5) | copy-start | bytes 52
  1327.0 5.7 copy-start.6
  1327.0 5.7 copy-start.7
where the time goes:
time: 1360 us; the launch traced here: 1350 us
  loops' own time  642 us (47%)
  other arithmetic  235 us (17%)
  local copies, waits for them, and re-layouts  212 us (16%)
  matrix products  161 us (12%)
  blocking collectives  75.7 us (6%)
  starting transfers between devices  22.2 us (2%)
    another operation x3, loops' own time, far_translate(): lax.scan(step_fn, jnp.zeros((size_x * size_y * size_z, 512), jnp.float32)...  554 us
    dot_general x88, matrix products, matmul(): jnp.dot(left, right, precision=highest, preferred_element_type=jnp.float32)  155 us
    another operation x1, loops' own time, translation_tables(): return lax.map(one_table, jnp.arange(27, dtype=jnp.int32))  88.1 us
    all_gather x1, blocking collectives, body(): gathered = lax.all_gather(first_piece, ('gx', 'gy'), axis=0, tiled=True)  75.7 us
    gather x28, other arithmetic, node_grid(): points[counter % 4]  65.8 us
    gather x28, other arithmetic, node_grid(): points[counter // 16]  65.6 us
    dynamic_slice x108, local copies, waits for them, and re-layouts, translation_tables(): return lax.map(one_table, jnp.arange(27, dtype=jnp.int32))  63.8 us
    slice x81, local copies, waits for them, and re-layouts, step_fn(): offset[2] + 1  50.2 us
  transfers between devices with their start and end apart: 8, of which 0 were waited for; matrix products, arithmetic and copies ran while one was open for 43% of the time, Pallas kernels for 0%

commit v1 on v0

v1 whole, which is shorter than its diff:
```python
import functools

import jax
import jax.numpy as jnp
import ml_dtypes
import numpy as np
from jax import lax
from jax.experimental import pallas as pl
from jax.experimental.pallas import tpu as pltpu
from jax.sharding import PartitionSpec as P

MESH = pl.DeviceIdType.MESH
F32 = jnp.float32
BF16 = jnp.bfloat16
DIRS = [(ox, oy) for ox in (-1, 0, 1) for oy in (-1, 0, 1) if (ox, oy) != (0, 0)]
ROWS = (1, 2, 3, -1, -2, -3)
TILES = 25


def nodes():
    return np.cos((2.0 * np.arange(4) + 1.0) * np.pi / 8.0)


def cubic():
    t = nodes()
    t2, t3 = 2 * t * t - 1, 4 * t**3 - 3 * t
    return np.stack([0.25 - 0.5 * t2, 0.5 * t - 1.5 * t3, t2, 2 * t3])


def split(x):
    hi = x.astype(ml_dtypes.bfloat16)
    lo = (x - hi.astype(np.float64)).astype(ml_dtypes.bfloat16)
    return hi, lo


def constants():
    t = nodes()
    c = cubic()
    shifted = (t[None, :] + 2.0 * np.arange(2)[:, None] - 1.0) / 2.0
    f = sum(c[k][None, None, :] * shifted[:, :, None] ** k for k in range(4))
    up = np.einsum("xia,yjb,zkc->xyzijkabc", f, f, f).reshape(2, 2, 2, 64, 64)
    uf = up.transpose(2, 4, 0, 1, 3).reshape(128, 256)
    uf = np.concatenate(split(uf), 0)
    u2 = up.transpose(0, 1, 2, 4, 3).reshape(2, 256, 64)
    u2 = np.concatenate(split(u2), 1)
    dn = up.reshape(4, 128, 64)
    dn = np.concatenate(split(dn), 1)
    n = np.arange(64)
    na, nb, nc = n // 16, n // 4 % 4, n % 4
    lane = np.arange(TILES * 128)
    pair, ln = lane // 64, lane % 64
    dx, dy = pair // 7 - 3, pair % 7 - 3
    lxy = np.zeros((TILES, 8, 128))
    lxy[:, 0] = (dx + t[na[ln]] / 2).reshape(TILES, 128)
    lxy[:, 1] = (dy + t[nb[ln]] / 2).reshape(TILES, 128)
    lxy[:, 2] = ((abs(dx) <= 1) & (abs(dy) <= 1)).reshape(TILES, 128)
    rxy = np.broadcast_to(np.stack([t[na] / 2, t[nb] / 2])[:, :, None], (2, 64, 128))
    sub = np.arange(8)
    l128 = np.arange(128)
    z2 = np.stack(
        [
            (dz + t[l128 % 4][None, :] / 2 - t[sub % 4][:, None] / 2) ** 2
            for dz in range(-3, 4)
        ]
    )
    w = np.zeros((3, 8, 128))
    for level, start, length in ((0, 0, 64), (1, 64, 16), (2, 80, 16)):
        for i, dz in enumerate(range(-3, 4)):
            for l in range(start, start + length):
                z = (l - start) % 16
                if z % 2**level or not 0 <= z + dz * 2**level < 16:
                    continue
                odd = (z >> level) % 2
                if (dz == 3 and odd) or (dz == -3 and not odd):
                    continue
                w[level, i, l] = 0.5**level
    pc = np.zeros((3, 4, 8, 128))
    for k in range(4):
        pc[0, k] = c[k][sub % 4][:, None]
        pc[1, k] = c[k][sub // 4][:, None]
        pc[2, k] = c[k][2 + sub // 4][:, None]
    l3 = np.zeros((8, 128))
    l3[0] = t[na[l128 % 64]] / 2
    l3[1] = t[nb[l128 % 64]] / 2
    f32 = [x.astype(np.float32) for x in (lxy, rxy, z2, w, pc, l3)]
    return [uf, u2, dn] + f32


def pair_split(x):
    hi = x.astype(BF16)
    lo = (x - hi.astype(F32)).astype(BF16)
    return hi, lo


def wide(x):
    return jnp.concatenate(pair_split(x), 1)


def folded(product, rows):
    return product[:rows, :128] + product[:rows, 128:] + product[rows:, :128] + product[rows:, 128:]


def dot(left, right):
    return jnp.dot(left, right, preferred_element_type=F32)


def kernel(
    count_x, count_y,
    own_ref, uf_ref, u2_ref, dn_ref, lxy_ref, rxy_ref, z2_ref, w_ref, pc_ref, l3_ref,
    out_ref,
    halo, moments, near_rows, rows, coarse, sources, targets, sums, table, table3, right, right3,
    product, bq, leaf,
    halo_s, halo_r, mom_s, mom_r, g_s, g_r, row_s, row_r, coarse_s, coarse_r,
):
    ix = lax.axis_index("gx")
    iy = lax.axis_index("gy")
    lane = lax.broadcasted_iota(jnp.int32, (8, 128), 1)
    lane64 = lax.broadcasted_iota(jnp.int32, (64, 128), 1)
    row64 = lax.broadcasted_iota(jnp.int32, (64, 128), 0)
    eye = row64 == lane64 % 64
    c = cubic()

    def remote(src, dst, send, recv, dx, dy):
        device = (lax.rem(ix + dx + count_x, count_x), lax.rem(iy + dy + count_y, count_y))
        return pltpu.make_async_remote_copy(
            src_ref=src, dst_ref=dst, send_sem=send, recv_sem=recv,
            device_id=device, device_id_type=MESH,
        )

    barrier = pltpu.get_barrier_semaphore()

    def greet(dx, dy):
        device = (lax.rem(ix + dx + count_x, count_x), lax.rem(iy + dy + count_y, count_y))
        pl.semaphore_signal(barrier, inc=1, device_id=device, device_id_type=MESH)

    for ox, oy in DIRS:
        greet(ox, oy)

    @pl.loop(1, count_y)
    def _(k):
        greet(0, k)

    @pl.loop(1, count_x)
    def _(k):
        greet(k, 0)

    def basis(column, k):
        x = 2.0 * halo[column, 0, k : k + 1, :] - 1.0
        y = 2.0 * halo[column, 1, k : k + 1, :] - 1.0
        z = 2.0 * halo[column, 2, k : k + 1, :] - 1.0

        def poly(i, u):
            return ((pc_ref[i, 3] * u + pc_ref[i, 2]) * u + pc_ref[i, 1]) * u + pc_ref[i, 0]

        along_z = poly(0, z)
        low, high = poly(1, y) * along_z, poly(2, y) * along_z
        pieces = []
        for a in range(4):
            s = ((float(c[3, a]) * x + float(c[2, a])) * x + float(c[1, a])) * x + float(c[0, a])
            pieces += [s * low, s * high]
        return jnp.concatenate(pieces, 0)

    def column_of(cx, cy):
        return (1 + cx) * 4 + 1 + cy

    for cx in range(2):
        for cy in range(2):
            halo[column_of(cx, cy)] = own_ref[cx, cy]
    half_row = lax.broadcasted_iota(jnp.int32, (128, 128), 0) // 64
    half_lane = lax.broadcasted_iota(jnp.int32, (128, 128), 1)
    parity = (half_row == half_lane % 2).astype(F32).astype(BF16)
    halves = (half_row == half_lane // 64).astype(F32).astype(BF16)
    leaf[...] = jnp.zeros((64, 128), F32)

    @pl.loop(0, 4)
    def _(col):
        column = (1 + col // 2) * 4 + 1 + col % 2
        for k in range(8):
            value = basis(column, k) * halo[column, 3, k : k + 1, :]
            hi, lo = pair_split(value)
            bq[64 * k : 64 * k + 64] = hi
            bq[512 + 64 * k : 576 + 64 * k] = lo
        summed = dot(bq[...], parity)
        total = leaf[...]
        for k in range(8):
            here = (lane64 % 64) // 2 == col * 8 + k
            total = jnp.where(
                here,
                summed[64 * k : 64 * k + 64] + summed[512 + 64 * k : 576 + 64 * k],
                total,
            )
        leaf[...] = total

    own = leaf[...]
    moments[4] = jnp.where(lane64[:32] < 64, own[:32], own[32:])
    stacked = jnp.concatenate(
        [own] + [pltpu.roll(own, 128 - 16 * col, 1) for col in range(1, 4)], 0
    )
    first = folded(dot(uf_ref[...], wide(stacked)), 128)
    first = first[:64] + pltpu.roll(first[64:], 127, 1)
    first = jnp.where((lane64 < 16) & (lane64 % 2 == 0), first, 0.0)
    first = first[:32] + pltpu.roll(first[32:], 1, 1)
    near_rows[iy] = pltpu.roll(first, 16 * iy, 1)

    pl.semaphore_wait(barrier, len(DIRS) + count_y - 1 + count_x - 1)

    gy_copies = []
    for k in range(1, count_y):
        copy = remote(near_rows.at[iy], near_rows.at[iy], g_s.at[k], g_r.at[k], 0, k)
        copy.start()
        gy_copies.append(copy)
    halo_copies, moment_copies = [], []
    for d, (ox, oy) in enumerate(DIRS):
        take_x = {1: [2], -1: [1], 0: [1, 2]}[ox]
        put_x = {1: [0], -1: [3], 0: [1, 2]}[ox]
        take_y = {1: (2, 1), -1: (1, 1), 0: (1, 2)}[oy]
        put_y = {1: 0, -1: 3, 0: 1}[oy]
        for i, (a, b) in enumerate(zip(take_x, put_x)):
            copy = remote(
                halo.at[pl.ds(a * 4 + take_y[0], take_y[1])],
                halo.at[pl.ds(b * 4 + put_y, take_y[1])],
                halo_s.at[2 * d + i], halo_r.at[2 * d + i], ox, oy,
            )
            copy.start()
            halo_copies.append(copy)
    for d, (ox, oy) in enumerate(DIRS):
        slot = (1 - ox) * 3 + 1 - oy
        copy = remote(moments.at[4], moments.at[slot], mom_s.at[d], mom_r.at[d], ox, oy)
        copy.start()
        moment_copies.append(copy)

    @pl.loop(0, TILES)
    def _(j):
        gap_x = lxy_ref[j, 0:1, :] - rxy_ref[0]
        gap_y = lxy_ref[j, 1:2, :] - rxy_ref[1]
        adjacent = jnp.broadcast_to(lxy_ref[j, 2:3, :], (64, 128)) > 0.5
        plane = gap_x * gap_x + gap_y * gap_y
        at = pl.ds(pl.multiple_of(j * 128, 128), 128)
        for i in range(7):
            value = lax.rsqrt(plane + jnp.concatenate([z2_ref[i]] * 8, 0))
            if i in (2, 3, 4):
                value = jnp.where(adjacent, 0.0, value)
            hi, lo = pair_split(value)
            table[64 * i : 64 * i + 64, at] = hi
            table[448 + 64 * i : 512 + 64 * i, at] = lo

    @pl.loop(0, count_x // 4)
    def _(j):
        apart = (j - ix // 4).astype(F32)
        side = (lane64 // 64 - iy // 4).astype(F32)
        gap_x = apart + l3_ref[0:1, :] - rxy_ref[0]
        gap_y = side + l3_ref[1:2, :] - rxy_ref[1]
        adjacent = jnp.maximum(jnp.abs(side), jnp.abs(apart)) <= 1.0
        plane = gap_x * gap_x + gap_y * gap_y
        at = pl.ds(pl.multiple_of(j * 128, 128), 128)
        for i in range(3):
            value = lax.rsqrt(plane + jnp.concatenate([z2_ref[i + 2]] * 8, 0))
            value = jnp.where(adjacent, 0.0, value)
            hi, lo = pair_split(value)
            table3[64 * i : 64 * i + 64, at] = hi
            table3[192 + 64 * i : 256 + 64 * i, at] = lo

    for copy in gy_copies:
        copy.wait_recv()
    row = near_rows[0]
    for k in range(1, count_y):
        row = row + near_rows[k]
    rows[ix] = row
    full = jnp.concatenate([row, pltpu.roll(row, 127, 1)], 0)
    full = jnp.where(lane64 % 2 == 0, full, 0.0)

    def part(source, which, step_z, step_y):
        o = folded(dot(u2_ref[which], wide(source)), 256)
        return (
            o[:64]
            + pltpu.roll(o[64:128], 128 - step_z, 1)
            + pltpu.roll(o[128:192], 128 - step_y, 1)
            + pltpu.roll(o[192:], 128 - step_z - step_y, 1)
        )

    second = part(full, ix % 2, 2, 16)
    second = jnp.where((lane64 // 16 % 2 == 0) & (lane64 % 4 == 0), second, 0.0)
    third = part(second, ix // 2 % 2, 4, 32)
    third = jnp.where((lane64 // 16 % 4 == 0) & (lane64 % 8 == 0), third, 0.0)
    packed = second[:16] + pltpu.roll(third[:16], 16, 1)
    for g in range(1, 4):
        at = slice(16 * g, 16 * g + 16)
        packed = packed + pltpu.roll(second[at], g, 1) + pltpu.roll(third[at], 16 + g, 1)
    coarse[ix] = packed

    row_copies = []
    for i, dx in enumerate(ROWS):
        copy = remote(rows.at[ix], rows.at[ix], row_s.at[i], row_r.at[i], dx, 0)
        copy.start()
        row_copies.append(copy)

    @pl.loop(1, count_x)
    def _(k):
        remote(coarse.at[ix], coarse.at[ix], coarse_s.at[k], coarse_r.at[k], k, 0).start()

    for col in range(4):
        column = column_of(col // 2, col % 2)
        for comp in range(3):
            value = halo[column, comp]
            if comp == 0:
                value = value + float(col // 2)
            if comp == 1:
                value = value + float(col % 2)
            if comp == 2:
                k2 = lax.broadcasted_iota(jnp.int32, (8, 128), 0)
                value = value + (2 * k2 + lane // 64).astype(F32)
            turned = value.T
            for k in range(8):
                spread = jnp.broadcast_to(turned[:, k : k + 1], (128, 128))
                targets[col * 8 + k, comp] = jnp.where(lane64 < 64, spread[:64], spread[64:])

    for copy in halo_copies:
        copy.wait_recv()

    inside_x = [ix > 0, None, None, ix < count_x - 1]
    inside_y = [iy > 0, None, None, iy < count_y - 1]
    sub = lax.broadcasted_iota(jnp.int32, (8, 128), 0)
    for wx in range(4):
        for wy in range(4):
            column = wx * 4 + wy
            for comp in range(4):
                value = halo[column, comp]
                if comp == 0:
                    value = value + float(wx - 1)
                if comp == 1:
                    value = value + float(wy - 1)
                if comp == 2:
                    value = value + (2 * sub + lane // 64).astype(F32)
                if comp == 3:
                    for inside in (inside_x[wx], inside_y[wy]):
                        if inside is not None:
                            value = value * inside.astype(F32)
                turned = pltpu.roll(value, 64, 1)
                below = jnp.where(lane < 64, pltpu.roll(turned, 1, 0), turned)
                above = jnp.where(lane < 64, turned, pltpu.roll(turned, 7, 0))
                if comp == 3:
                    below = jnp.where((lane < 64) & (sub == 0), 0.0, below)
                    above = jnp.where((lane >= 64) & (sub == 7), 0.0, above)
                sources[column, 0, comp] = below
                sources[column, 1, comp] = value
                sources[column, 2, comp] = above

    @pl.loop(0, 32)
    def _(block):
        col, k = block // 8, block % 8
        cx, cy = col // 2, col % 2
        tx, ty, tz = targets[block, 0], targets[block, 1], targets[block, 2]
        total = jnp.zeros((64, 128), F32)
        for dx in range(3):
            for dy in range(3):
                column = (cx + dx) * 4 + cy + dy
                for dz in range(3):
                    sx = sources[column, dz, 0, pl.ds(k, 1), :]
                    sy = sources[column, dz, 1, pl.ds(k, 1), :]
                    sz = sources[column, dz, 2, pl.ds(k, 1), :]
                    q = sources[column, dz, 3, pl.ds(k, 1), :]
                    gx, gy, gz = tx - sx, ty - sy, tz - sz
                    inverse = lax.rsqrt(gx * gx + gy * gy + gz * gz)
                    if (dx, dy, dz) == (1, 1, 1):
                        inverse = jnp.where(eye, 0.0, inverse)
                    total = total + inverse * q
        sums[block] = total

    for copy in moment_copies:
        copy.wait_recv()
    for copy in row_copies:
        copy.wait_recv()

    @pl.loop(1, count_x)
    def _(k):
        remote(coarse.at[ix], coarse.at[ix], coarse_s.at[k], coarse_r.at[k], k, 0).wait_recv()

    def unpacked(value, start):
        return jnp.concatenate(
            [pltpu.roll(value, lax.rem(start - g + 128, 128), 1) for g in range(4)], 0
        )

    for j in range(count_x // 4):
        group = coarse[4 * j] + coarse[4 * j + 1] + coarse[4 * j + 2] + coarse[4 * j + 3]
        third = unpacked(group, jnp.int32(112))
        right3[128 * j : 128 * j + 64] = wide(third)
        right3[128 * j + 64 : 128 * j + 128] = wide(pltpu.roll(third, 64, 1))
    o = folded(dot(table3[...], right3[...]), 192)
    local = o[64:128]
    local = local + jnp.where(lane64 == 0, pltpu.roll(o[128:], 120, 1), 0.0)
    local = local + jnp.where(lane64 == 8, pltpu.roll(o[:64], 8, 1), 0.0)
    local3 = jnp.where((lane64 < 16) & (lane64 % 8 == 0), 0.125 * local, 0.0)

    plain, crossed = {}, {}
    for ox in (-1, 0, 1):
        for oy in (-1, 0, 1):
            value = moments[(ox + 1) * 3 + oy + 1]
            turned = pltpu.roll(value, 64, 1)
            lane32 = lane64[:32]
            value = jnp.concatenate(
                [jnp.where(lane32 < 64, value, turned), jnp.where(lane32 < 64, turned, value)], 0
            )
            scale = F32(1.0)
            if ox:
                scale = scale * (ix > 0 if ox < 0 else ix < count_x - 1).astype(F32)
            if oy:
                scale = scale * (iy > 0 if oy < 0 else iy < count_y - 1).astype(F32)
            plain[ox, oy] = value * scale
    by_x = lane64 // 32 % 2
    by_y = lane64 // 16 % 2

    def swap_y(value):
        return jnp.where(by_y == 0, pltpu.roll(value, 112, 1), pltpu.roll(value, 16, 1))

    def leaf_block(dx, dy):
        result = None
        for cx in range(2):
            for cy in range(2):
                ox, oy = (cx + dx) // 2, (cy + dy) // 2
                if abs(ox) > 1 or abs(oy) > 1:
                    continue
                value = plain[ox, oy]
                if dy % 2:
                    value = swap_y(value)
                if dx % 2:
                    value = pltpu.roll(value, 32, 1)
                mine = (by_x == cx) & (by_y == cy)
                value = jnp.where(mine, value, 0.0)
                result = value if result is None else result + value
        return result

    def within(value, count, step, odd):
        ok = (value >= 0) & (value < count)
        if step == 3:
            ok = ok & (odd == 0)
        if step == -3:
            ok = ok & (odd == 1)
        return ok.astype(F32)

    for dx in range(-3, 4):
        line = rows[lax.rem(ix + dx + count_x, count_x)]
        line = jnp.concatenate([line, pltpu.roll(line, 127, 1)], 0)
        line = pltpu.roll(line, lax.rem(64 - 16 * iy + 128, 128), 1)
        line = line * within(ix + dx, count_x, dx, ix % 2)
        x2 = ix // 2 + dx
        base = lax.rem(2 * x2 + 2 * count_x, count_x)
        pair = unpacked(coarse[base] + coarse[base + 1], lax.rem(80 - 32 * (iy // 2) + 128, 128))
        pair = pair * within(x2, count_x // 2, dx, ix // 2 % 2)
        for dy in range(-3, 4):
            one = pltpu.roll(line, (-16 * dy) % 128, 1) * within(iy + dy, count_y, dy, iy % 2)
            two = pltpu.roll(pair, (-32 * dy) % 128, 1)
            two = two * within(iy // 2 + dy, count_y // 2, dy, iy // 2 % 2)
            value = jnp.where(lane64 < 64, leaf_block(dx, dy), jnp.where(lane64 < 80, one, two))
            value = jnp.where(lane64 < 96, value, 0.0)
            at = ((dx + 3) * 7 + dy + 3) * 64
            right[at : at + 64] = wide(value)
    right[49 * 64 : 50 * 64] = jnp.zeros((64, 256), BF16)

    @pl.loop(0, 7)
    def _(j):
        at = pl.ds(pl.multiple_of(j * 128, 128), 128)
        product[at] = dot(table[at], right[...])

    far = jnp.zeros((64, 128), F32)
    for i in range(7):
        dz = i - 3
        o = product[64 * i : 64 * i + 64]
        o2 = product[448 + 64 * i : 512 + 64 * i]
        o = o[:, :128] + o[:, 128:] + o2[:, :128] + o2[:, 128:]
        for level in range(3):
            value = o if dz == 0 else pltpu.roll(o, (-dz * 2**level) % 128, 1)
            far = far + value * w_ref[level, i : i + 1, :]

    def down(source, which, step):
        o = folded(dot(dn_ref[which], wide(source)), 128)
        return jnp.where(lane64 % (2 * step) == 0, o[:64], pltpu.roll(o[64:], step, 1))

    low = lane64 < 16
    local2 = down(local3, ix // 2 % 2 * 2 + iy // 2 % 2, 4) + pltpu.roll(far, 48, 1)
    local2 = jnp.where(low & (lane64 % 4 == 0), local2, 0.0)
    local1 = down(local2, ix % 2 * 2 + iy % 2, 2) + pltpu.roll(far, 64, 1)
    local1 = jnp.where(low & (lane64 % 2 == 0), local1, 0.0)
    local0 = far
    for col in range(4):
        value = down(local1, col, 1)
        if col:
            value = pltpu.roll(value, 16 * col, 1)
        local0 = local0 + jnp.where(lane64 // 16 == col, value, 0.0)
    leaf[...] = local0

    @pl.loop(0, 4)
    def _(col):
        column = (1 + col // 2) * 4 + 1 + col % 2
        near = sums[pl.ds(pl.multiple_of(col * 8, 8), 8)].reshape(512, 128)
        hi, lo = pair_split(near)
        near = dot(hi, halves) + dot(lo, halves)
        here = pltpu.roll(leaf[...], lax.rem(128 - 16 * col, 128), 1)
        for k in range(8):
            spread = jnp.where(
                lane64 < 64,
                jnp.broadcast_to(here[:, 2 * k : 2 * k + 1], (64, 128)),
                jnp.broadcast_to(here[:, 2 * k + 1 : 2 * k + 2], (64, 128)),
            )
            both = basis(column, k) * spread
            both = both + jnp.where(eye, near[64 * k : 64 * k + 64], 0.0)
            out_ref[col, k : k + 1, :] = jnp.sum(both, 0, keepdims=True)

    for copy in gy_copies + halo_copies + moment_copies + row_copies:
        copy.wait_send()

    @pl.loop(1, count_x)
    def _(k):
        remote(coarse.at[ix], coarse.at[ix], coarse_s.at[k], coarse_r.at[k], k, 0).wait_send()


def solution(mesh):
    count_x, count_y = mesh.shape["gx"], mesh.shape["gy"]
    fixed = constants()
    vmem = pl.BlockSpec(memory_space=pltpu.VMEM)
    dma = pltpu.SemaphoreType.DMA
    call = pl.pallas_call(
        functools.partial(kernel, count_x, count_y),
        out_shape=jax.ShapeDtypeStruct((4, 8, 128), F32),
        in_specs=[vmem] * (1 + len(fixed)),
        out_specs=vmem,
        scratch_shapes=[
            pltpu.VMEM((16, 4, 8, 128), F32),
            pltpu.VMEM((9, 32, 128), F32),
            pltpu.VMEM((count_y, 32, 128), F32),
            pltpu.VMEM((count_x, 32, 128), F32),
            pltpu.VMEM((count_x, 16, 128), F32),
            pltpu.VMEM((16, 3, 4, 8, 128), F32),
            pltpu.VMEM((32, 3, 64, 128), F32),
            pltpu.VMEM((32, 64, 128), F32),
            pltpu.VMEM((896, TILES * 128), BF16),
            pltpu.VMEM((384, count_x // 4 * 128), BF16),
            pltpu.VMEM((TILES * 128, 256), BF16),
            pltpu.VMEM((count_x // 4 * 128, 256), BF16),
            pltpu.VMEM((896, 256), F32),
            pltpu.VMEM((1024, 128), BF16),
            pltpu.VMEM((64, 128), F32),
            dma((16,)),
            dma((16,)),
            dma((8,)),
            dma((8,)),
            dma((count_y,)),
            dma((count_y,)),
            dma((6,)),
            dma((6,)),
            dma((count_x,)),
            dma((count_x,)),
        ],
        compiler_params=pltpu.CompilerParams(
            collective_id=0, has_side_effects=True, vmem_limit_bytes=48 << 20
        ),
    )

    def body(offsets, charges):
        own = jnp.concatenate([offsets, charges[None]], 0)
        own = own.transpose(1, 2, 0, 3).reshape(2, 2, 4, 8, 128)
        return call(own, *fixed).reshape(2, 2, 1024)

    in_specs = (P(None, "gx", "gy", None), P("gx", "gy", None))
    out_specs = P("gx", "gy", None)
    return jax.shard_map(body, mesh=mesh, in_specs=in_specs, out_specs=out_specs, check_vma=False)
```

time: 1360 us -> 49 us (0.04)
  loops' own time: 642 us -> 0 us
  other arithmetic: 235 us -> 0.89 us
  local copies, waits for them, and re-layouts: 212 us -> 6.44 us
  matrix products: 161 us -> 0 us
  blocking collectives: 75.7 us -> 0 us
  Pallas kernels: 0 us -> 41.2 us
  starting transfers between devices: 22.2 us -> 0 us
    another operation x4 -> x0, loops' own time: 642 us -> none  [the longest x3 554 us: far_translate(): lax.scan(step_fn, jnp.zeros((size_x * size_y * size_z, 512), jnp.float32)...]
    dot_general x90 -> x0, matrix products: 161 us -> none  [the longest x88 155 us: matmul(): jnp.dot(left, right, precision=highest, preferred_element_type=jnp.float32)]
    gather x56 -> x0, other arithmetic: 131 us -> none  [the longest x28 65.8 us: node_grid(): points[counter % 4]]
    all_gather x1 -> x0, blocking collectives: 75.7 us -> none  [body(): gathered = lax.all_gather(first_piece, ('gx', 'gy'), axis=0, tiled=True)]
    dynamic_slice x164 -> x0, local copies, waits for them, and re-layouts: 65.7 us -> none  [the longest x108 63.8 us: translation_tables(): return lax.map(one_table, jnp.arange(27, dtype=jnp.int32))]
    reduce_sum x31 -> x0, other arithmetic: 52.1 us -> none  [the longest x27 30.7 us: translation(): distance = jnp.sqrt(jnp.sum(separation * separation, -1))]
    slice x87 -> x0, local copies, waits for them, and re-layouts: 51.3 us -> none  [the longest x81 50.2 us: step_fn(): offset[2] + 1]
    pallas_call x0 -> x1, Pallas kernels: none -> 41.2 us  [body(): return call(own, *fixed).reshape(2, 2, 1024)]
  transfers between devices with their start and end apart: 8 -> 0, of which waited for: 0 -> 0; matrix products, arithmetic and copies ran while one was open for 43% -> 0% of each run, Pallas kernels for 0% -> 0%
where the time goes in v1:
time: 49 us; the launch traced here: 48.6 us
  Pallas kernels  41.2 us (84%)
  local copies, waits for them, and re-layouts  6.44 us (13%)
  other arithmetic  0.89 us (2%)
    pallas_call x1, Pallas kernels, body(): return call(own, *fixed).reshape(2, 2, 1024)  41.2 us
    unnamed x18, local copies, waits for them, and re-layouts  5.77 us

profile of v1, /device:TPU:1, one launch (start us, length us, event | category | flops | bytes accessed | tf_op | source)
XLA Modules:
  0.0 48.6 jit_solution(8684323703765736251)
XLA Ops:
  0.0 0.0 copy-start
  0.0 0.9 %maximum_bitcast_fusion = f32[2,2,4,1024]{3,1,0,2:T(2,128)S(1)} fusion(f32[1,2,2,1024]{3,2,1,0:T(2,128)} %bitcast.5, f32[3,2,2,1024]{3,2,1,0:T(2,128)} %param.11), kind=kLoop, calls=%fused_computation | loop fusion | flops 16384 | bytes 131072 | tf_op jit(solution)/shard_map/transpose | solution.py:560
  0.9 0.0 copy-start.2
  0.9 0.1 reshape.8
  1.0 0.0 copy-start.8
  1.0 0.0 copy-done
  1.0 0.8 %copy-done.2 = bf16[256,256]{1,0:T(8,128)(2,1)S(1)} copy-done((bf16[256,256]{1,0:T(8,128)(2,1)S(1)}, bf16[256,256]{1,0:T(8,128)(2,1)}, u32[]{:S(2)}) %copy-start.2) | copy-done | bytes 131096
  1.8 0.0 copy-done.8
  1.8 0.0 copy-start.1
  1.8 0.9 %copy-done.1 = bf16[2,512,64]{2,1,0:T(8,128)(2,1)S(1)} copy-done((bf16[2,512,64]{2,1,0:T(8,128)(2,1)S(1)}, bf16[2,512,64]{2,1,0:T(8,128)(2,1)}, u32[]{:S(2)}) %copy-start.1) | copy-done | bytes 131096
  2.8 0.0 copy-start.3
  2.8 0.9 %copy-done.3 = f32[25,8,128]{2,1,0:T(8,128)S(1)} copy-done((f32[25,8,128]{2,1,0:T(8,128)S(1)}, f32[25,8,128]{2,1,0:T(8,128)}, u32[]{:S(2)}) %copy-start.3) | copy-done | bytes 102424
  3.7 0.0 copy-start.4
  3.7 0.8 %copy-done.4 = f32[2,64,128]{2,1,0:T(8,128)S(1)} copy-done((f32[2,64,128]{2,1,0:T(8,128)S(1)}, f32[2,64,128]{2,1,0:T(8,128)}, u32[]{:S(2)}) %copy-start.4) | copy-done | bytes 65560
  4.5 0.0 copy-start.5
  4.5 0.8 %copy-done.5 = f32[3,4,8,128]{3,2,1,0:T(8,128)S(1)} copy-done((f32[3,4,8,128]{3,2,1,0:T(8,128)S(1)}, f32[3,4,8,128]{3,2,1,0:T(8,128)}, u32[]{:S(2)}) %copy-start.5) | copy-done | bytes 49176
  5.3 0.0 copy-start.6
  5.3 0.7 %copy-done.6 = f32[7,8,128]{2,1,0:T(8,128)S(1)} copy-done((f32[7,8,128]{2,1,0:T(8,128)S(1)}, f32[7,8,128]{2,1,0:T(8,128)}, u32[]{:S(2)}) %copy-start.6) | copy-done | bytes 28696
  6.1 0.0 copy-start.7
  6.1 0.7 %copy-done.7 = f32[3,8,128]{2,1,0:T(8,128)S(1)} copy-done((f32[3,8,128]{2,1,0:T(8,128)S(1)}, f32[3,8,128]{2,1,0:T(8,128)}, u32[]{:S(2)}) %copy-start.7) | copy-done | bytes 12312
  6.8 41.2 %shard_map.109 = f32[4,8,128]{2,1,0:T(8,128)S(1)} custom-call(f32[2,2,4,8,128]{4,3,2,1,0:T(8,128)S(1)} %copy.13.own_ref, bf16[256,256]{1,0:T(8,128)(2,1)S(1)} %copy-done.2, bf16[2,512,64]{2,1,0:T(8,128)(2,1)S(1)} %copy-done.1, bf16[4,256,64]{2,1,0:T(8,128)(2,1)S(1)} %copy-done, f32[25,8,128]{2,1,0:T(8,128)S(1)} %copy-done.3, f32[2,64,128]{2,1,0:T(8,128)S(1)} %copy-done.4, ...), custom_call_target="tpu_custom_call" | custom-call | tf_op jit(solution)/shard_map/pallas_call | solution.py:561
  48.0 0.6 %reshape.7 = f32[2,2,1024]{2,1,0:T(2,128)} reshape(f32[4,8,128]{2,1,0:T(8,128)S(1)} %shard_map.109) | data formatting | bytes 32768 | tf_op jit(solution)/shard_map/reshape | solution.py:561
  (1 shorter events, 0.0 us)
Async XLA Ops:
  0.0 1.0 %copy-start = (bf16[4,256,64]{2,1,0:T(8,128)(2,1)S(1)}, bf16[4,256,64]{2,1,0:T(8,128)(2,1)}, u32[]{:S(2)}) copy-start(bf16[4,256,64]{2,1,0:T(8,128)(2,1)} %constant.20.clone.dn_ref) | copy-start | bytes 393220
  0.9 0.9 %copy-start.2 = (bf16[256,256]{1,0:T(8,128)(2,1)S(1)}, bf16[256,256]{1,0:T(8,128)(2,1)}, u32[]{:S(2)}) copy-start(bf16[256,256]{1,0:T(8,128)(2,1)} %constant.18.clone.uf_ref) | copy-start | bytes 393220
  1.0 0.9 %copy-start.8 = (f32[8,128]{1,0:T(8,128)S(1)}, f32[8,128]{1,0:T(8,128)}, u32[]{:S(2)}) copy-start(f32[8,128]{1,0:T(8,128)} %constant.26.clone.l3_ref) | copy-start | bytes 12292
  1.8 1.0 %copy-start.1 = (bf16[2,512,64]{2,1,0:T(8,128)(2,1)S(1)}, bf16[2,512,64]{2,1,0:T(8,128)(2,1)}, u32[]{:S(2)}) copy-start(bf16[2,512,64]{2,1,0:T(8,128)(2,1)} %constant.19.clone.u2_ref) | copy-start | bytes 393220
  2.8 0.9 %copy-start.3 = (f32[25,8,128]{2,1,0:T(8,128)S(1)}, f32[25,8,128]{2,1,0:T(8,128)}, u32[]{:S(2)}) copy-start(f32[25,8,128]{2,1,0:T(8,128)} %constant.21.clone.lxy_ref) | copy-start | bytes 307204
  3.7 0.8 %copy-start.4 = (f32[2,64,128]{2,1,0:T(8,128)S(1)}, f32[2,64,128]{2,1,0:T(8,128)}, u32[]{:S(2)}) copy-start(f32[2,64,128]{2,1,0:T(8,128)} %constant.22.clone.rxy_ref) | copy-start | bytes 196612
  4.5 0.8 %copy-start.5 = (f32[3,4,8,128]{3,2,1,0:T(8,128)S(1)}, f32[3,4,8,128]{3,2,1,0:T(8,128)}, u32[]{:S(2)}) copy-start(f32[3,4,8,128]{3,2,1,0:T(8,128)} %constant.25.clone.pc_ref) | copy-start | bytes 147460
  5.3 0.7 %copy-start.6 = (f32[7,8,128]{2,1,0:T(8,128)S(1)}, f32[7,8,128]{2,1,0:T(8,128)}, u32[]{:S(2)}) copy-start(f32[7,8,128]{2,1,0:T(8,128)} %constant.23.clone.z2_ref) | copy-start | bytes 86020
  6.1 0.7 %copy-start.7 = (f32[3,8,128]{2,1,0:T(8,128)S(1)}, f32[3,8,128]{2,1,0:T(8,128)}, u32[]{:S(2)}) copy-start(f32[3,8,128]{2,1,0:T(8,128)} %constant.24.clone.w_ref) | copy-start | bytes 36868

commit v2 on v1

--- a/solution.py
+++ b/solution.py
@@ -82,8 +82,8 @@
     l3 = np.zeros((8, 128))
     l3[0] = t[na[l128 % 64]] / 2
     l3[1] = t[nb[l128 % 64]] / 2
-    f32 = [x.astype(np.float32) for x in (lxy, rxy, z2, w, pc, l3)]
-    return [uf, u2, dn] + f32
+    flat = np.concatenate([x.reshape(-1, 128) for x in (pc, lxy, rxy, z2, w, l3)], 0)
+    return [flat.astype(np.float32), uf, u2, dn]
 
 
 def pair_split(x):
@@ -106,12 +106,27 @@
 
 def kernel(
     count_x, count_y,
-    own_ref, uf_ref, u2_ref, dn_ref, lxy_ref, rxy_ref, z2_ref, w_ref, pc_ref, l3_ref,
+    off_hbm, charge_hbm, flat_hbm, uf_hbm, u2_hbm, dn_hbm,
     out_ref,
-    halo, moments, near_rows, rows, coarse, sources, targets, sums, table, table3, right, right3,
-    product, bq, leaf,
-    halo_s, halo_r, mom_s, mom_r, g_s, g_r, row_s, row_r, coarse_s, coarse_r,
+    off_ref, charge_ref, flat, uf_ref, u2_ref, dn_ref,
+    halo, moments, near_rows, rows, coarse, pieces, source, charge, target, sums, near,
+    table, table3, right, right3, product, bq, leaf,
+    load_s, halo_s, halo_r, mom_s, mom_r, g_s, g_r, row_s, row_r, coarse_s, coarse_r,
 ):
+    loads = [
+        pltpu.make_async_copy(src, dst, load_s.at[i])
+        for i, (src, dst) in enumerate(
+            [(off_hbm, off_ref), (charge_hbm, charge_ref), (flat_hbm, flat)]
+            + [(uf_hbm, uf_ref), (u2_hbm, u2_ref), (dn_hbm, dn_ref)]
+        )
+    ]
+    for load in loads:
+        load.start()
+    at_lxy = 96
+    at_rxy = at_lxy + 8 * TILES
+    at_z2 = at_rxy + 128
+    at_w = at_z2 + 56
+    at_l3 = at_w + 24
     ix = lax.axis_index("gx")
     iy = lax.axis_index("gy")
     lane = lax.broadcasted_iota(jnp.int32, (8, 128), 1)
@@ -150,7 +165,8 @@
         z = 2.0 * halo[column, 2, k : k + 1, :] - 1.0
 
         def poly(i, u):
-            return ((pc_ref[i, 3] * u + pc_ref[i, 2]) * u + pc_ref[i, 1]) * u + pc_ref[i, 0]
+            p = [flat[32 * i + 8 * e : 32 * i + 8 * e + 8] for e in range(4)]
+            return ((p[3] * u + p[2]) * u + p[1]) * u + p[0]
 
         along_z = poly(0, z)
         low, high = poly(1, y) * along_z, poly(2, y) * along_z
@@ -163,9 +179,15 @@
     def column_of(cx, cy):
         return (1 + cx) * 4 + 1 + cy
 
+    for load in loads[:3]:
+        load.wait()
     for cx in range(2):
         for cy in range(2):
-            halo[column_of(cx, cy)] = own_ref[cx, cy]
+            for k in range(8):
+                at = slice(128 * k, 128 * k + 128)
+                for comp in range(3):
+                    halo[column_of(cx, cy), comp, k : k + 1] = off_ref[comp, cx, cy : cy + 1, at]
+                halo[column_of(cx, cy), 3, k : k + 1] = charge_ref[cx, cy : cy + 1, at]
     half_row = lax.broadcasted_iota(jnp.int32, (128, 128), 0) // 64
     half_lane = lax.broadcasted_iota(jnp.int32, (128, 128), 1)
     parity = (half_row == half_lane % 2).astype(F32).astype(BF16)
@@ -191,6 +213,8 @@
             )
         leaf[...] = total
 
+    for load in loads[3:]:
+        load.wait()
     own = leaf[...]
     moments[4] = jnp.where(lane64[:32] < 64, own[:32], own[32:])
     stacked = jnp.concatenate(
@@ -231,13 +255,14 @@
 
     @pl.loop(0, TILES)
     def _(j):
-        gap_x = lxy_ref[j, 0:1, :] - rxy_ref[0]
-        gap_y = lxy_ref[j, 1:2, :] - rxy_ref[1]
-        adjacent = jnp.broadcast_to(lxy_ref[j, 2:3, :], (64, 128)) > 0.5
+        line = flat[pl.ds(pl.multiple_of(at_lxy + 8 * j, 8), 8)]
+        gap_x = line[0:1] - flat[at_rxy : at_rxy + 64]
+        gap_y = line[1:2] - flat[at_rxy + 64 : at_rxy + 128]
+        adjacent = jnp.broadcast_to(line[2:3], (64, 128)) > 0.5
         plane = gap_x * gap_x + gap_y * gap_y
         at = pl.ds(pl.multiple_of(j * 128, 128), 128)
         for i in range(7):
-            value = lax.rsqrt(plane + jnp.concatenate([z2_ref[i]] * 8, 0))
+            value = lax.rsqrt(plane + jnp.concatenate([flat[at_z2 + 8 * i : at_z2 + 8 * i + 8]] * 8, 0))
             if i in (2, 3, 4):
                 value = jnp.where(adjacent, 0.0, value)
             hi, lo = pair_split(value)
@@ -248,13 +273,13 @@
     def _(j):
         apart = (j - ix // 4).astype(F32)
         side = (lane64 // 64 - iy // 4).astype(F32)
-        gap_x = apart + l3_ref[0:1, :] - rxy_ref[0]
-        gap_y = side + l3_ref[1:2, :] - rxy_ref[1]
+        gap_x = apart + flat[at_l3 : at_l3 + 1] - flat[at_rxy : at_rxy + 64]
+        gap_y = side + flat[at_l3 + 1 : at_l3 + 2] - flat[at_rxy + 64 : at_rxy + 128]
         adjacent = jnp.maximum(jnp.abs(side), jnp.abs(apart)) <= 1.0
         plane = gap_x * gap_x + gap_y * gap_y
         at = pl.ds(pl.multiple_of(j * 128, 128), 128)
         for i in range(3):
-            value = lax.rsqrt(plane + jnp.concatenate([z2_ref[i + 2]] * 8, 0))
+            value = lax.rsqrt(plane + jnp.concatenate([flat[at_z2 + 8 * i + 16 : at_z2 + 8 * i + 24]] * 8, 0))
             value = jnp.where(adjacent, 0.0, value)
             hi, lo = pair_split(value)
             table3[64 * i : 64 * i + 64, at] = hi
@@ -298,73 +323,147 @@
     def _(k):
         remote(coarse.at[ix], coarse.at[ix], coarse_s.at[k], coarse_r.at[k], k, 0).start()
 
-    for col in range(4):
-        column = column_of(col // 2, col % 2)
-        for comp in range(3):
-            value = halo[column, comp]
-            if comp == 0:
-                value = value + float(col // 2)
-            if comp == 1:
-                value = value + float(col % 2)
-            if comp == 2:
-                k2 = lax.broadcasted_iota(jnp.int32, (8, 128), 0)
-                value = value + (2 * k2 + lane // 64).astype(F32)
-            turned = value.T
-            for k in range(8):
-                spread = jnp.broadcast_to(turned[:, k : k + 1], (128, 128))
-                targets[col * 8 + k, comp] = jnp.where(lane64 < 64, spread[:64], spread[64:])
+    sub = lax.broadcasted_iota(jnp.int32, (8, 128), 0)
+    first_term = (sub == 0) | (sub == 1) | (sub == 3)
+    second_term = (sub == 2) | (sub == 4)
+    half = (lane // 64).astype(F32)
+
+    def three(value):
+        a = value.astype(BF16).astype(F32)
+        rest = value - a
+        b = rest.astype(BF16).astype(F32)
+        return [a, b, rest - b]
+
+    def features(column, wx, wy, both):
+        x = halo[column, 0] + (wx - 1.0)
+        y = halo[column, 1] + (wy - 1.0)
+        z = halo[column, 2] + (half - 1.0)
+        plane = x * x + y * y
+        parts = three(x) + three(y) + three(z) + three(plane + z * z)
+        if both:
+            beside = z + (2.0 - 4.0 * half)
+            parts += three(beside) + three(plane + beside * beside)
+        for i, part in enumerate(parts):
+            pieces[i] = part
+
+    def spread(i, k):
+        return jnp.broadcast_to(pieces[i, k : k + 1], (8, 128))
+
+    def chosen(i, k, six, seven, terms):
+        a, b, c = (spread(i + e, k) for e in range(3))
+        value = jnp.where(terms[0], a, jnp.where(terms[1], b, c))
+        return jnp.where(sub == 6, six, jnp.where(sub == 7, seven, value))
+
+    zero8 = jnp.zeros((8, 128), F32)
+    one8 = jnp.ones((8, 128), F32)
+    t_terms = ((sub == 0) | (sub == 2) | (sub == 5), (sub == 1) | (sub == 4))
+    s_terms = (first_term, second_term)
+    scale8 = jnp.where(sub < 6, -2.0, 1.0)
+
+    @pl.loop(0, 4)
+    def _(col):
+        cx, cy = col // 2, col % 2
+        features((1 + cx) * 4 + 1 + cy, cx.astype(F32), cy.astype(F32), False)
+        for k in range(0, 8, 2):
+            turned = []
+            for e in (k, k + 1):
+                tiles = [
+                    chosen(0, e, one8, one8, t_terms),
+                    chosen(3, e, one8, spread(9, e), t_terms),
+                    chosen(6, e, spread(10, e), spread(11, e), t_terms),
+                ]
+                tiles = jnp.concatenate([t * scale8 for t in tiles] + [zero8], 0)
+                turned.append((tiles, pltpu.roll(tiles, 64, 1)))
+            lane32 = lane64[:32] < 64
+            upper = jnp.where(lane32, turned[0][0], turned[1][1])
+            lower = jnp.where(lane32, turned[0][1], turned[1][0])
+            stack = jnp.concatenate([upper, lower], 0).T.astype(BF16)
+            target[col * 8 + k] = stack[:64]
+            target[col * 8 + k + 1] = stack[64:]
 
     for copy in halo_copies:
         copy.wait_recv()
 
-    inside_x = [ix > 0, None, None, ix < count_x - 1]
-    inside_y = [iy > 0, None, None, iy < count_y - 1]
-    sub = lax.broadcasted_iota(jnp.int32, (8, 128), 0)
-    for wx in range(4):
-        for wy in range(4):
-            column = wx * 4 + wy
-            for comp in range(4):
-                value = halo[column, comp]
-                if comp == 0:
-                    value = value + float(wx - 1)
-                if comp == 1:
-                    value = value + float(wy - 1)
-                if comp == 2:
-                    value = value + (2 * sub + lane // 64).astype(F32)
-                if comp == 3:
-                    for inside in (inside_x[wx], inside_y[wy]):
-                        if inside is not None:
-                            value = value * inside.astype(F32)
-                turned = pltpu.roll(value, 64, 1)
-                below = jnp.where(lane < 64, pltpu.roll(turned, 1, 0), turned)
-                above = jnp.where(lane < 64, turned, pltpu.roll(turned, 7, 0))
-                if comp == 3:
-                    below = jnp.where((lane < 64) & (sub == 0), 0.0, below)
-                    above = jnp.where((lane >= 64) & (sub == 7), 0.0, above)
-                sources[column, 0, comp] = below
-                sources[column, 1, comp] = value
-                sources[column, 2, comp] = above
-
-    @pl.loop(0, 32)
-    def _(block):
+    outside = jnp.where(lax.broadcasted_iota(jnp.int32, (32, 128), 0) == 6, 16384.0, 0.0)
+    lane32 = lane64[:32] < 64
+    left_half = lane32
+    outside_low = jnp.where(left_half, outside, 0.0).astype(BF16)
+    outside_high = jnp.where(left_half, 0.0, outside).astype(BF16)
+
+    @pl.loop(0, 16)
+    def _(column):
+        wx, wy = column // 4, column % 4
+        features(column, wx.astype(F32) - 1.0, wy.astype(F32) - 1.0, True)
+        at_x, at_y = 2 * ix + wx - 1, 2 * iy + wy - 1
+        inside = (at_x >= 0) & (at_x < 2 * count_x) & (at_y >= 0) & (at_y < 2 * count_y)
+        q = halo[column, 3] * inside.astype(F32)
+        after = jnp.where(sub == 7, 0.0, pltpu.roll(q, 7, 0))
+        before = jnp.where(sub == 0, 0.0, pltpu.roll(q, 1, 0))
+        charge[column, 0] = jnp.where(lane < 64, q, before)
+        charge[column, 1] = q
+        charge[column, 2] = jnp.where(lane < 64, after, q)
+        source[column, 9, 2] = outside_low
+        source[column, 0, 3] = outside_high
+        for k in range(8):
+            own_tiles = [
+                chosen(0, k, spread(9, k), spread(10, k), s_terms),
+                chosen(3, k, spread(11, k), one8, s_terms),
+                chosen(6, k, one8, one8, s_terms),
+                zero8,
+            ]
+            beside_tiles = [
+                jnp.where(sub == 6, spread(15, k), jnp.where(sub == 7, spread(16, k), own_tiles[0])),
+                jnp.where(sub == 6, spread(17, k), own_tiles[1]),
+                chosen(12, k, one8, one8, s_terms),
+                zero8,
+            ]
+            for e, tiles in enumerate((own_tiles, beside_tiles)):
+                tiles = jnp.concatenate(tiles, 0)
+                source[column, k + 1, 2 * e] = jnp.where(left_half, tiles, 0.0).astype(BF16)
+                source[column, k + 1, 2 * e + 1] = jnp.where(left_half, 0.0, tiles).astype(BF16)
+
+    def near_block(block, carry):
         col, k = block // 8, block % 8
         cx, cy = col // 2, col % 2
-        tx, ty, tz = targets[block, 0], targets[block, 1], targets[block, 2]
-        total = jnp.zeros((64, 128), F32)
-        for dx in range(3):
-            for dy in range(3):
-                column = (cx + dx) * 4 + cy + dy
-                for dz in range(3):
-                    sx = sources[column, dz, 0, pl.ds(k, 1), :]
-                    sy = sources[column, dz, 1, pl.ds(k, 1), :]
-                    sz = sources[column, dz, 2, pl.ds(k, 1), :]
-                    q = sources[column, dz, 3, pl.ds(k, 1), :]
-                    gx, gy, gz = tx - sx, ty - sy, tz - sz
-                    inverse = lax.rsqrt(gx * gx + gy * gy + gz * gz)
-                    if (dx, dy, dz) == (1, 1, 1):
-                        inverse = jnp.where(eye, 0.0, inverse)
-                    total = total + inverse * q
-        sums[block] = total
+        mine = target[block]
+        straight = jnp.zeros((64, 128), F32)
+        crossed = jnp.zeros((64, 128), F32)
+        columns = [(cx + dx) * 4 + cy + dy for dx in range(3) for dy in range(3)]
+
+        def side(column, a, b):
+            return jnp.concatenate([source[column, a[0], a[1]], source[column, b[0], b[1]]], 0)
+
+        def row_of(column, dz):
+            return charge[column, dz, pl.ds(k, 1), :]
+
+        for column in columns:
+            above = side(column, (k + 1, 1), (k + 2, 2))
+            below = side(column, (k, 3), (k + 1, 0))
+            inverse = lax.rsqrt(dot(mine, jnp.concatenate([above, below], 1)))
+            crossed = crossed + inverse[:, :128] * row_of(column, 2)
+            crossed = crossed + inverse[:, 128:] * row_of(column, 0)
+        for i in range(0, 9, 2):
+            group = columns[i : i + 2]
+            both = [side(column, (k + 1, 0), (k + 1, 1)) for column in group]
+            inverse = lax.rsqrt(dot(mine, jnp.concatenate(both, 1)))
+            for e, column in enumerate(group):
+                value = inverse[:, 128 * e : 128 * e + 128]
+                if i + e == 4:
+                    value = jnp.where(eye, 0.0, value)
+                straight = straight + value * row_of(column, 1)
+        sums[block] = straight + pltpu.roll(crossed, 64, 1)
+        return carry
+
+    lax.fori_loop(0, 32, near_block, 0, unroll=2)
+
+    @pl.loop(0, 4)
+    def _(col):
+        value = sums[pl.ds(pl.multiple_of(col * 8, 8), 8)].reshape(512, 128)
+        hi, lo = pair_split(value)
+        value = dot(hi, halves) + dot(lo, halves)
+        for k in range(8):
+            mine = jnp.where(eye, value[64 * k : 64 * k + 64], 0.0)
+            near[col, k : k + 1] = jnp.sum(mine, 0, keepdims=True)
 
     for copy in moment_copies:
         copy.wait_recv()
@@ -456,10 +555,7 @@
             right[at : at + 64] = wide(value)
     right[49 * 64 : 50 * 64] = jnp.zeros((64, 256), BF16)
 
-    @pl.loop(0, 7)
-    def _(j):
-        at = pl.ds(pl.multiple_of(j * 128, 128), 128)
-        product[at] = dot(table[at], right[...])
+    product[...] = dot(table[...], right[...])
 
     far = jnp.zeros((64, 128), F32)
     for i in range(7):
@@ -469,7 +565,7 @@
         o = o[:, :128] + o[:, 128:] + o2[:, :128] + o2[:, 128:]
         for level in range(3):
             value = o if dz == 0 else pltpu.roll(o, (-dz * 2**level) % 128, 1)
-            far = far + value * w_ref[level, i : i + 1, :]
+            far = far + value * flat[at_w + 8 * level + i : at_w + 8 * level + i + 1]
 
     def down(source, which, step):
         o = folded(dot(dn_ref[which], wide(source)), 128)
@@ -491,9 +587,6 @@
     @pl.loop(0, 4)
     def _(col):
         column = (1 + col // 2) * 4 + 1 + col % 2
-        near = sums[pl.ds(pl.multiple_of(col * 8, 8), 8)].reshape(512, 128)
-        hi, lo = pair_split(near)
-        near = dot(hi, halves) + dot(lo, halves)
         here = pltpu.roll(leaf[...], lax.rem(128 - 16 * col, 128), 1)
         for k in range(8):
             spread = jnp.where(
@@ -502,8 +595,12 @@
                 jnp.broadcast_to(here[:, 2 * k + 1 : 2 * k + 2], (64, 128)),
             )
             both = basis(column, k) * spread
-            both = both + jnp.where(eye, near[64 * k : 64 * k + 64], 0.0)
-            out_ref[col, k : k + 1, :] = jnp.sum(both, 0, keepdims=True)
+            near[col, k : k + 1] = jnp.sum(both, 0, keepdims=True) + near[col, k : k + 1]
+
+    for col in range(4):
+        for k in range(8):
+            at = slice(128 * k, 128 * k + 128)
+            out_ref[col // 2, col % 2 : col % 2 + 1, at] = near[col, k : k + 1]
 
     for copy in gy_copies + halo_copies + moment_copies + row_copies:
         copy.wait_send()
@@ -517,21 +614,31 @@
     count_x, count_y = mesh.shape["gx"], mesh.shape["gy"]
     fixed = constants()
     vmem = pl.BlockSpec(memory_space=pltpu.VMEM)
+    hbm = pl.BlockSpec(memory_space=pltpu.HBM)
     dma = pltpu.SemaphoreType.DMA
     call = pl.pallas_call(
         functools.partial(kernel, count_x, count_y),
-        out_shape=jax.ShapeDtypeStruct((4, 8, 128), F32),
-        in_specs=[vmem] * (1 + len(fixed)),
+        out_shape=jax.ShapeDtypeStruct((2, 2, 1024), F32),
+        in_specs=[hbm] * (2 + len(fixed)),
         out_specs=vmem,
         scratch_shapes=[
+            pltpu.VMEM((3, 2, 2, 1024), F32),
+            pltpu.VMEM((2, 2, 1024), F32),
+            pltpu.VMEM(fixed[0].shape, F32),
+            pltpu.VMEM(fixed[1].shape, BF16),
+            pltpu.VMEM(fixed[2].shape, BF16),
+            pltpu.VMEM(fixed[3].shape, BF16),
             pltpu.VMEM((16, 4, 8, 128), F32),
             pltpu.VMEM((9, 32, 128), F32),
             pltpu.VMEM((count_y, 32, 128), F32),
             pltpu.VMEM((count_x, 32, 128), F32),
             pltpu.VMEM((count_x, 16, 128), F32),
-            pltpu.VMEM((16, 3, 4, 8, 128), F32),
-            pltpu.VMEM((32, 3, 64, 128), F32),
+            pltpu.VMEM((18, 8, 128), F32),
+            pltpu.VMEM((16, 10, 4, 32, 128), BF16),
+            pltpu.VMEM((16, 3, 8, 128), F32),
+            pltpu.VMEM((32, 64, 64), BF16),
             pltpu.VMEM((32, 64, 128), F32),
+            pltpu.VMEM((4, 8, 128), F32),
             pltpu.VMEM((896, TILES * 128), BF16),
             pltpu.VMEM((384, count_x // 4 * 128), BF16),
             pltpu.VMEM((TILES * 128, 256), BF16),
@@ -539,6 +646,7 @@
             pltpu.VMEM((896, 256), F32),
             pltpu.VMEM((1024, 128), BF16),
             pltpu.VMEM((64, 128), F32),
+            dma((6,)),
             dma((16,)),
             dma((16,)),
             dma((8,)),
@@ -551,14 +659,12 @@
             dma((count_x,)),
         ],
         compiler_params=pltpu.CompilerParams(
-            collective_id=0, has_side_effects=True, vmem_limit_bytes=48 << 20
+            collective_id=0, has_side_effects=True, vmem_limit_bytes=64 << 20
         ),
     )
 
     def body(offsets, charges):
-        own = jnp.concatenate([offsets, charges[None]], 0)
-        own = own.transpose(1, 2, 0, 3).reshape(2, 2, 4, 8, 128)
-        return call(own, *fixed).reshape(2, 2, 1024)
+        return call(offsets, charges, *fixed)
 
     in_specs = (P(None, "gx", "gy", None), P("gx", "gy", None))
     out_specs = P("gx", "gy", None)

time: 49 us -> 37.4 us (0.76)
  Pallas kernels: 41.2 us -> 35.9 us
  local copies, waits for them, and re-layouts: 6.44 us -> 1.32 us
  other arithmetic: 0.89 us -> 0 us
    pallas_call x1, Pallas kernels: 41.2 us -> 35.9 us  [body(): return call(offsets, charges, *fixed)]
    unnamed x18 -> x1, local copies, waits for them, and re-layouts: 5.77 us -> 1.32 us
    transpose x1 -> x0, other arithmetic: 0.89 us -> none  [body(): own = own.transpose(1, 2, 0, 3).reshape(2, 2, 4, 8, 128)]
    reshape x3 -> x0, local copies, waits for them, and re-layouts: 0.68 us -> none  [the longest x1 0.62 us: body(): return call(own, *fixed).reshape(2, 2, 1024)]
where the time goes in v2:
time: 37.4 us; the launch traced here: 37.2 us
  Pallas kernels  35.9 us (96%)
  local copies, waits for them, and re-layouts  1.32 us (4%)
    pallas_call x1, Pallas kernels, body(): return call(offsets, charges, *fixed)  35.9 us
    unnamed x1, local copies, waits for them, and re-layouts  1.32 us

profile of v2, /device:TPU:1, one launch (start us, length us, event | category | flops | bytes accessed | tf_op | source)
XLA Modules:
  0.0 37.2 jit_solution(1442268333126378802)
XLA Ops:
  0.0 35.9 %shard_map.64 = f32[2,2,1024]{2,1,0:T(2,128)} custom-call(f32[3,2,2,1024]{3,2,1,0:T(2,128)} %off_hbm.1, f32[2,2,1024]{2,1,0:T(2,128)} %charge_hbm.1, f32[512,128]{1,0:T(8,128)} %constant.8.clone.flat_hbm, bf16[256,256]{1,0:T(8,128)(2,1)} %constant.9.clone.uf_hbm, bf16[2,512,64]{2,1,0:T(8,128)(2,1)} %constant.10.clone.u2_hbm, ...), custom_call_target="tpu_custom_call" | custom-call | tf_op jit(solution)/shard_map/pallas_call | solution.py:667
  35.9 1.3 %copy.8 = f32[2,2,1024]{2,1,0:T(2,128)} copy(f32[2,2,1024]{2,1,0:T(2,128)} %shard_map.64) | data formatting | bytes 32768

commit v3 on v2

--- a/solution.py
+++ b/solution.py
@@ -45,45 +45,7 @@
     u2 = np.concatenate(split(u2), 1)
     dn = up.reshape(4, 128, 64)
     dn = np.concatenate(split(dn), 1)
-    n = np.arange(64)
-    na, nb, nc = n // 16, n // 4 % 4, n % 4
-    lane = np.arange(TILES * 128)
-    pair, ln = lane // 64, lane % 64
-    dx, dy = pair // 7 - 3, pair % 7 - 3
-    lxy = np.zeros((TILES, 8, 128))
-    lxy[:, 0] = (dx + t[na[ln]] / 2).reshape(TILES, 128)
-    lxy[:, 1] = (dy + t[nb[ln]] / 2).reshape(TILES, 128)
-    lxy[:, 2] = ((abs(dx) <= 1) & (abs(dy) <= 1)).reshape(TILES, 128)
-    rxy = np.broadcast_to(np.stack([t[na] / 2, t[nb] / 2])[:, :, None], (2, 64, 128))
-    sub = np.arange(8)
-    l128 = np.arange(128)
-    z2 = np.stack(
-        [
-            (dz + t[l128 % 4][None, :] / 2 - t[sub % 4][:, None] / 2) ** 2
-            for dz in range(-3, 4)
-        ]
-    )
-    w = np.zeros((3, 8, 128))
-    for level, start, length in ((0, 0, 64), (1, 64, 16), (2, 80, 16)):
-        for i, dz in enumerate(range(-3, 4)):
-            for l in range(start, start + length):
-                z = (l - start) % 16
-                if z % 2**level or not 0 <= z + dz * 2**level < 16:
-                    continue
-                odd = (z >> level) % 2
-                if (dz == 3 and odd) or (dz == -3 and not odd):
-                    continue
-                w[level, i, l] = 0.5**level
-    pc = np.zeros((3, 4, 8, 128))
-    for k in range(4):
-        pc[0, k] = c[k][sub % 4][:, None]
-        pc[1, k] = c[k][sub // 4][:, None]
-        pc[2, k] = c[k][2 + sub // 4][:, None]
-    l3 = np.zeros((8, 128))
-    l3[0] = t[na[l128 % 64]] / 2
-    l3[1] = t[nb[l128 % 64]] / 2
-    flat = np.concatenate([x.reshape(-1, 128) for x in (pc, lxy, rxy, z2, w, l3)], 0)
-    return [flat.astype(np.float32), uf, u2, dn]
+    return [uf, u2, dn]
 
 
 def pair_split(x):
@@ -106,24 +68,23 @@
 
 def kernel(
     count_x, count_y,
-    off_hbm, charge_hbm, flat_hbm, uf_hbm, u2_hbm, dn_hbm,
+    off_hbm, charge_hbm, uf_hbm, u2_hbm, dn_hbm,
     out_ref,
     off_ref, charge_ref, flat, uf_ref, u2_ref, dn_ref,
     halo, moments, near_rows, rows, coarse, pieces, source, charge, target, sums, near,
-    table, table3, right, right3, product, bq, leaf,
-    load_s, halo_s, halo_r, mom_s, mom_r, g_s, g_r, row_s, row_r, coarse_s, coarse_r,
+    table, table3, right, right3, product, bq, leaf, bases,
+    load_s, send_s, recv_s,
 ):
     loads = [
         pltpu.make_async_copy(src, dst, load_s.at[i])
         for i, (src, dst) in enumerate(
-            [(off_hbm, off_ref), (charge_hbm, charge_ref), (flat_hbm, flat)]
+            [(off_hbm, off_ref), (charge_hbm, charge_ref)]
             + [(uf_hbm, uf_ref), (u2_hbm, u2_ref), (dn_hbm, dn_ref)]
         )
     ]
     for load in loads:
         load.start()
-    at_lxy = 96
-    at_rxy = at_lxy + 8 * TILES
+    at_rxy = 96
     at_z2 = at_rxy + 128
     at_w = at_z2 + 56
     at_l3 = at_w + 24
@@ -133,7 +94,36 @@
     lane64 = lax.broadcasted_iota(jnp.int32, (64, 128), 1)
     row64 = lax.broadcasted_iota(jnp.int32, (64, 128), 0)
     eye = row64 == lane64 % 64
+    sub = lax.broadcasted_iota(jnp.int32, (8, 128), 0)
     c = cubic()
+    t = nodes()
+
+    def pick(index, values):
+        result = jnp.full(index.shape, float(values[3]), F32)
+        for e in (2, 1, 0):
+            result = jnp.where(index == e, float(values[e]), result)
+        return result
+
+    for i, index in enumerate((sub % 4, sub // 4, 2 + sub // 4)):
+        for e in range(4):
+            flat[32 * i + 8 * e : 32 * i + 8 * e + 8] = pick(index, c[e])
+    flat[at_rxy : at_rxy + 64] = 0.5 * pick(row64 // 16, t)
+    flat[at_rxy + 64 : at_rxy + 128] = 0.5 * pick(row64 // 4 % 4, t)
+    gap_z = 0.5 * (pick(lane % 4, t) - pick(sub % 4, t))
+    for i in range(7):
+        gap = gap_z + (i - 3.0)
+        flat[at_z2 + 8 * i : at_z2 + 8 * i + 8] = gap * gap
+    for level, start, length in ((0, 0, 64), (1, 64, 16), (2, 80, 16)):
+        z = lane % 16
+        seen = z + (sub - 3) * 2**level
+        odd = (z // 2**level) % 2
+        ok = (z % 2**level == 0) & (seen >= 0) & (seen < 16) & (sub < 7)
+        ok = ok & (lane >= start) & (lane < start + length)
+        ok = ok & ((sub < 6) | (odd == 0)) & ((sub > 0) | (odd == 1))
+        flat[at_w + 8 * level : at_w + 8 * level + 8] = jnp.where(ok, 0.5**level, 0.0)
+    lane_x = 0.5 * pick(lane % 64 // 16, t)
+    lane_y = 0.5 * pick(lane // 4 % 4, t)
+    flat[at_l3 : at_l3 + 8] = jnp.where(sub == 0, lane_x, lane_y)
 
     def remote(src, dst, send, recv, dx, dy):
         device = (lax.rem(ix + dx + count_x, count_x), lax.rem(iy + dy + count_y, count_y))
@@ -151,114 +141,20 @@
     for ox, oy in DIRS:
         greet(ox, oy)
 
-    @pl.loop(1, count_y)
-    def _(k):
+    for k in range(1, count_y):
         greet(0, k)
-
-    @pl.loop(1, count_x)
-    def _(k):
+    for k in range(1, count_x):
         greet(k, 0)
-
-    def basis(column, k):
-        x = 2.0 * halo[column, 0, k : k + 1, :] - 1.0
-        y = 2.0 * halo[column, 1, k : k + 1, :] - 1.0
-        z = 2.0 * halo[column, 2, k : k + 1, :] - 1.0
-
-        def poly(i, u):
-            p = [flat[32 * i + 8 * e : 32 * i + 8 * e + 8] for e in range(4)]
-            return ((p[3] * u + p[2]) * u + p[1]) * u + p[0]
-
-        along_z = poly(0, z)
-        low, high = poly(1, y) * along_z, poly(2, y) * along_z
-        pieces = []
-        for a in range(4):
-            s = ((float(c[3, a]) * x + float(c[2, a])) * x + float(c[1, a])) * x + float(c[0, a])
-            pieces += [s * low, s * high]
-        return jnp.concatenate(pieces, 0)
-
-    def column_of(cx, cy):
-        return (1 + cx) * 4 + 1 + cy
-
-    for load in loads[:3]:
-        load.wait()
-    for cx in range(2):
-        for cy in range(2):
-            for k in range(8):
-                at = slice(128 * k, 128 * k + 128)
-                for comp in range(3):
-                    halo[column_of(cx, cy), comp, k : k + 1] = off_ref[comp, cx, cy : cy + 1, at]
-                halo[column_of(cx, cy), 3, k : k + 1] = charge_ref[cx, cy : cy + 1, at]
-    half_row = lax.broadcasted_iota(jnp.int32, (128, 128), 0) // 64
-    half_lane = lax.broadcasted_iota(jnp.int32, (128, 128), 1)
-    parity = (half_row == half_lane % 2).astype(F32).astype(BF16)
-    halves = (half_row == half_lane // 64).astype(F32).astype(BF16)
-    leaf[...] = jnp.zeros((64, 128), F32)
-
-    @pl.loop(0, 4)
-    def _(col):
-        column = (1 + col // 2) * 4 + 1 + col % 2
-        for k in range(8):
-            value = basis(column, k) * halo[column, 3, k : k + 1, :]
-            hi, lo = pair_split(value)
-            bq[64 * k : 64 * k + 64] = hi
-            bq[512 + 64 * k : 576 + 64 * k] = lo
-        summed = dot(bq[...], parity)
-        total = leaf[...]
-        for k in range(8):
-            here = (lane64 % 64) // 2 == col * 8 + k
-            total = jnp.where(
-                here,
-                summed[64 * k : 64 * k + 64] + summed[512 + 64 * k : 576 + 64 * k],
-                total,
-            )
-        leaf[...] = total
-
-    for load in loads[3:]:
-        load.wait()
-    own = leaf[...]
-    moments[4] = jnp.where(lane64[:32] < 64, own[:32], own[32:])
-    stacked = jnp.concatenate(
-        [own] + [pltpu.roll(own, 128 - 16 * col, 1) for col in range(1, 4)], 0
-    )
-    first = folded(dot(uf_ref[...], wide(stacked)), 128)
-    first = first[:64] + pltpu.roll(first[64:], 127, 1)
-    first = jnp.where((lane64 < 16) & (lane64 % 2 == 0), first, 0.0)
-    first = first[:32] + pltpu.roll(first[32:], 1, 1)
-    near_rows[iy] = pltpu.roll(first, 16 * iy, 1)
-
-    pl.semaphore_wait(barrier, len(DIRS) + count_y - 1 + count_x - 1)
-
-    gy_copies = []
-    for k in range(1, count_y):
-        copy = remote(near_rows.at[iy], near_rows.at[iy], g_s.at[k], g_r.at[k], 0, k)
-        copy.start()
-        gy_copies.append(copy)
-    halo_copies, moment_copies = [], []
-    for d, (ox, oy) in enumerate(DIRS):
-        take_x = {1: [2], -1: [1], 0: [1, 2]}[ox]
-        put_x = {1: [0], -1: [3], 0: [1, 2]}[ox]
-        take_y = {1: (2, 1), -1: (1, 1), 0: (1, 2)}[oy]
-        put_y = {1: 0, -1: 3, 0: 1}[oy]
-        for i, (a, b) in enumerate(zip(take_x, put_x)):
-            copy = remote(
-                halo.at[pl.ds(a * 4 + take_y[0], take_y[1])],
-                halo.at[pl.ds(b * 4 + put_y, take_y[1])],
-                halo_s.at[2 * d + i], halo_r.at[2 * d + i], ox, oy,
-            )
-            copy.start()
-            halo_copies.append(copy)
-    for d, (ox, oy) in enumerate(DIRS):
-        slot = (1 - ox) * 3 + 1 - oy
-        copy = remote(moments.at[4], moments.at[slot], mom_s.at[d], mom_r.at[d], ox, oy)
-        copy.start()
-        moment_copies.append(copy)
 
     @pl.loop(0, TILES)
     def _(j):
-        line = flat[pl.ds(pl.multiple_of(at_lxy + 8 * j, 8), 8)]
-        gap_x = line[0:1] - flat[at_rxy : at_rxy + 64]
-        gap_y = line[1:2] - flat[at_rxy + 64 : at_rxy + 128]
-        adjacent = jnp.broadcast_to(line[2:3], (64, 128)) > 0.5
+        dx = [(2 * j + e) // 7 - 3 for e in range(2)]
+        dy = [(2 * j + e) % 7 - 3 for e in range(2)]
+        dx, dy = (jnp.where(lane < 64, v[0], v[1]).astype(F32) for v in (dx, dy))
+        gap_x = (dx + lane_x)[:1] - flat[at_rxy : at_rxy + 64]
+        gap_y = (dy + lane_y)[:1] - flat[at_rxy + 64 : at_rxy + 128]
+        adjacent = jnp.maximum(jnp.abs(dx), jnp.abs(dy))[:1]
+        adjacent = jnp.broadcast_to(adjacent, (64, 128)) <= 1.0
         plane = gap_x * gap_x + gap_y * gap_y
         at = pl.ds(pl.multiple_of(j * 128, 128), 128)
         for i in range(7):
@@ -285,8 +181,104 @@
             table3[64 * i : 64 * i + 64, at] = hi
             table3[192 + 64 * i : 256 + 64 * i, at] = lo
 
-    for copy in gy_copies:
-        copy.wait_recv()
+    def basis(column, k):
+        x = 2.0 * halo[column, 0, k : k + 1, :] - 1.0
+        y = 2.0 * halo[column, 1, k : k + 1, :] - 1.0
+        z = 2.0 * halo[column, 2, k : k + 1, :] - 1.0
+
+        def poly(i, u):
+            p = [flat[32 * i + 8 * e : 32 * i + 8 * e + 8] for e in range(4)]
+            return ((p[3] * u + p[2]) * u + p[1]) * u + p[0]
+
+        along_z = poly(0, z)
+        low, high = poly(1, y) * along_z, poly(2, y) * along_z
+        pieces = []
+        for a in range(4):
+            s = ((float(c[3, a]) * x + float(c[2, a])) * x + float(c[1, a])) * x + float(c[0, a])
+            pieces += [s * low, s * high]
+        return jnp.concatenate(pieces, 0)
+
+    def column_of(cx, cy):
+        return (1 + cx) * 4 + 1 + cy
+
+    for load in loads[:2]:
+        load.wait()
+    for cx in range(2):
+        for cy in range(2):
+            for k in range(8):
+                at = slice(128 * k, 128 * k + 128)
+                for comp in range(3):
+                    halo[column_of(cx, cy), comp, k : k + 1] = off_ref[comp, cx, cy : cy + 1, at]
+                halo[column_of(cx, cy), 3, k : k + 1] = charge_ref[cx, cy : cy + 1, at]
+    half_row = lax.broadcasted_iota(jnp.int32, (128, 128), 0) // 64
+    half_lane = lax.broadcasted_iota(jnp.int32, (128, 128), 1)
+    parity = (half_row == half_lane % 2).astype(F32).astype(BF16)
+    halves = (half_row == half_lane // 64).astype(F32).astype(BF16)
+    leaf[...] = jnp.zeros((64, 128), F32)
+
+    @pl.loop(0, 4, unroll=True)
+    def _(col):
+        column = (1 + col // 2) * 4 + 1 + col % 2
+        for k in range(8):
+            value = basis(column, k)
+            bases[8 * col + k] = value
+            value = value * halo[column, 3, k : k + 1, :]
+            hi, lo = pair_split(value)
+            bq[col, 64 * k : 64 * k + 64] = hi
+            bq[col, 512 + 64 * k : 576 + 64 * k] = lo
+        summed = dot(bq[col], parity)
+        total = leaf[...]
+        for k in range(8):
+            here = (lane64 % 64) // 2 == col * 8 + k
+            total = jnp.where(
+                here,
+                summed[64 * k : 64 * k + 64] + summed[512 + 64 * k : 576 + 64 * k],
+                total,
+            )
+        leaf[...] = total
+
+    for load in loads[2:]:
+        load.wait()
+    own = leaf[...]
+    moments[4] = jnp.where(lane64[:32] < 64, own[:32], own[32:])
+    stacked = jnp.concatenate(
+        [own] + [pltpu.roll(own, 128 - 16 * col, 1) for col in range(1, 4)], 0
+    )
+    first = folded(dot(uf_ref[...], wide(stacked)), 128)
+    first = first[:64] + pltpu.roll(first[64:], 127, 1)
+    first = jnp.where((lane64 < 16) & (lane64 % 2 == 0), first, 0.0)
+    first = first[:32] + pltpu.roll(first[32:], 1, 1)
+    near_rows[iy] = pltpu.roll(first, 16 * iy, 1)
+
+    pl.semaphore_wait(barrier, len(DIRS) + count_y - 1 + count_x - 1)
+
+    ROW, HALO, LEAF, LINE, COARSE = range(5)
+    buffers = (near_rows, halo, moments, rows, coarse)
+    counts = (count_y - 1, 12, 8, 6, count_x - 1)
+
+    def send(kind, index, at, dx, dy):
+        buffer = buffers[kind]
+        sems = (send_s.at[kind], recv_s.at[kind])
+        remote(buffer.at[index], buffer.at[at], *sems, dx, dy).start()
+
+    def all_of(kind):
+        part = buffers[kind].at[pl.ds(0, counts[kind])]
+        return remote(part, part, send_s.at[kind], recv_s.at[kind], 1, 1)
+
+    for k in range(1, count_y):
+        send(ROW, iy, iy, 0, k)
+    for ox, oy in DIRS:
+        take_x = {1: [2], -1: [1], 0: [1, 2]}[ox]
+        put_x = {1: [0], -1: [3], 0: [1, 2]}[ox]
+        take_y = {1: (2, 1), -1: (1, 1), 0: (1, 2)}[oy]
+        put_y = {1: 0, -1: 3, 0: 1}[oy]
+        for a, b in zip(take_x, put_x):
+            at = (pl.ds(a * 4 + take_y[0], take_y[1]), pl.ds(b * 4 + put_y, take_y[1]))
+            send(HALO, *at, ox, oy)
+    for ox, oy in DIRS:
+        send(LEAF, 4, (1 - ox) * 3 + 1 - oy, ox, oy)
+
+    all_of(ROW).wait_recv()
     row = near_rows[0]
     for k in range(1, count_y):
         row = row + near_rows[k]
@@ -313,17 +305,11 @@
         packed = packed + pltpu.roll(second[at], g, 1) + pltpu.roll(third[at], 16 + g, 1)
     coarse[ix] = packed
 
-    row_copies = []
-    for i, dx in enumerate(ROWS):
-        copy = remote(rows.at[ix], rows.at[ix], row_s.at[i], row_r.at[i], dx, 0)
-        copy.start()
-        row_copies.append(copy)
-
-    @pl.loop(1, count_x)
-    def _(k):
-        remote(coarse.at[ix], coarse.at[ix], coarse_s.at[k], coarse_r.at[k], k, 0).start()
-
-    sub = lax.broadcasted_iota(jnp.int32, (8, 128), 0)
+    for k in range(1, count_x):
+        send(COARSE, ix, ix, k, 0)
+    for dx in ROWS:
+        send(LINE, ix, ix, dx, 0)
+
     first_term = (sub == 0) | (sub == 1) | (sub == 3)
     second_term = (sub == 2) | (sub == 4)
     half = (lane // 64).astype(F32)
@@ -344,13 +330,13 @@
             beside = z + (2.0 - 4.0 * half)
             parts += three(beside) + three(plane + beside * beside)
         for i, part in enumerate(parts):
-            pieces[i] = part
-
-    def spread(i, k):
-        return jnp.broadcast_to(pieces[i, k : k + 1], (8, 128))
-
-    def chosen(i, k, six, seven, terms):
-        a, b, c = (spread(i + e, k) for e in range(3))
+            pieces[column, i] = part
+
+    def spread(column, i, k):
+        return jnp.broadcast_to(pieces[column, i, k : k + 1], (8, 128))
+
+    def chosen(column, i, k, six, seven, terms):
+        a, b, c = (spread(column, i + e, k) for e in range(3))
         value = jnp.where(terms[0], a, jnp.where(terms[1], b, c))
         return jnp.where(sub == 6, six, jnp.where(sub == 7, seven, value))
 
@@ -360,17 +346,18 @@
     s_terms = (first_term, second_term)
     scale8 = jnp.where(sub < 6, -2.0, 1.0)
 
-    @pl.loop(0, 4)
+    @pl.loop(0, 4, unroll=True)
     def _(col):
         cx, cy = col // 2, col % 2
-        features((1 + cx) * 4 + 1 + cy, cx.astype(F32), cy.astype(F32), False)
+        column = (1 + cx) * 4 + 1 + cy
+        features(column, cx.astype(F32), cy.astype(F32), False)
         for k in range(0, 8, 2):
             turned = []
             for e in (k, k + 1):
                 tiles = [
-                    chosen(0, e, one8, one8, t_terms),
-                    chosen(3, e, one8, spread(9, e), t_terms),
-                    chosen(6, e, spread(10, e), spread(11, e), t_terms),
+                    chosen(column, 0, e, one8, one8, t_terms),
+                    chosen(column, 3, e, one8, spread(column, 9, e), t_terms),
+                    chosen(column, 6, e, spread(column, 10, e), spread(column, 11, e), t_terms),
                 ]
                 tiles = jnp.concatenate([t * scale8 for t in tiles] + [zero8], 0)
                 turned.append((tiles, pltpu.roll(tiles, 64, 1)))
@@ -381,8 +368,7 @@
             target[col * 8 + k] = stack[:64]
             target[col * 8 + k + 1] = stack[64:]
 
-    for copy in halo_copies:
-        copy.wait_recv()
+    all_of(HALO).wait_recv()
 
     outside = jnp.where(lax.broadcasted_iota(jnp.int32, (32, 128), 0) == 6, 16384.0, 0.0)
     lane32 = lane64[:32] < 64
@@ -390,7 +376,7 @@
     outside_low = jnp.where(left_half, outside, 0.0).astype(BF16)
     outside_high = jnp.where(left_half, 0.0, outside).astype(BF16)
 
-    @pl.loop(0, 16)
+    @pl.loop(0, 16, unroll=4)
     def _(column):
         wx, wy = column // 4, column % 4
         features(column, wx.astype(F32) - 1.0, wy.astype(F32) - 1.0, True)
@@ -406,15 +392,15 @@
         source[column, 0, 3] = outside_high
         for k in range(8):
             own_tiles = [
-                chosen(0, k, spread(9, k), spread(10, k), s_terms),
-                chosen(3, k, spread(11, k), one8, s_terms),
-                chosen(6, k, one8, one8, s_terms),
+                chosen(column, 0, k, spread(column, 9, k), spread(column, 10, k), s_terms),
+                chosen(column, 3, k, spread(column, 11, k), one8, s_terms),
+                chosen(column, 6, k, one8, one8, s_terms),
                 zero8,
             ]
             beside_tiles = [
-                jnp.where(sub == 6, spread(15, k), jnp.where(sub == 7, spread(16, k), own_tiles[0])),
-                jnp.where(sub == 6, spread(17, k), own_tiles[1]),
-                chosen(12, k, one8, one8, s_terms),
+                jnp.where(sub == 6, spread(column, 15, k), jnp.where(sub == 7, spread(column, 16, k), own_tiles[0])),
+                jnp.where(sub == 6, spread(column, 17, k), own_tiles[1]),
+                chosen(column, 12, k, one8, one8, s_terms),
                 zero8,
             ]
             for e, tiles in enumerate((own_tiles, beside_tiles)):
@@ -454,9 +440,9 @@
         sums[block] = straight + pltpu.roll(crossed, 64, 1)
         return carry
 
-    lax.fori_loop(0, 32, near_block, 0, unroll=2)
-
-    @pl.loop(0, 4)
+    lax.fori_loop(0, 32, near_block, 0, unroll=8)
+
+    @pl.loop(0, 4, unroll=True)
     def _(col):
         value = sums[pl.ds(pl.multiple_of(col * 8, 8), 8)].reshape(512, 128)
         hi, lo = pair_split(value)
@@ -465,14 +451,8 @@
             mine = jnp.where(eye, value[64 * k : 64 * k + 64], 0.0)
             near[col, k : k + 1] = jnp.sum(mine, 0, keepdims=True)
 
-    for copy in moment_copies:
-        copy.wait_recv()
-    for copy in row_copies:
-        copy.wait_recv()
-
-    @pl.loop(1, count_x)
-    def _(k):
-        remote(coarse.at[ix], coarse.at[ix], coarse_s.at[k], coarse_r.at[k], k, 0).wait_recv()
+    for kind in (LEAF, LINE, COARSE):
+        all_of(kind).wait_recv()
 
     def unpacked(value, start):
         return jnp.concatenate(
@@ -584,7 +564,7 @@
         local0 = local0 + jnp.where(lane64 // 16 == col, value, 0.0)
     leaf[...] = local0
 
-    @pl.loop(0, 4)
+    @pl.loop(0, 4, unroll=True)
     def _(col):
         column = (1 + col // 2) * 4 + 1 + col % 2
         here = pltpu.roll(leaf[...], lax.rem(128 - 16 * col, 128), 1)
@@ -594,7 +574,7 @@
                 jnp.broadcast_to(here[:, 2 * k : 2 * k + 1], (64, 128)),
                 jnp.broadcast_to(here[:, 2 * k + 1 : 2 * k + 2], (64, 128)),
             )
-            both = basis(column, k) * spread
+            both = bases[8 * col + k] * spread
             near[col, k : k + 1] = jnp.sum(both, 0, keepdims=True) + near[col, k : k + 1]
 
     for col in range(4):
@@ -602,12 +582,8 @@
             at = slice(128 * k, 128 * k + 128)
             out_ref[col // 2, col % 2 : col % 2 + 1, at] = near[col, k : k + 1]
 
-    for copy in gy_copies + halo_copies + moment_copies + row_copies:
-        copy.wait_send()
-
-    @pl.loop(1, count_x)
-    def _(k):
-        remote(coarse.at[ix], coarse.at[ix], coarse_s.at[k], coarse_r.at[k], k, 0).wait_send()
+    for kind in range(5):
+        all_of(kind).wait_send()
 
 
 def solution(mesh):
@@ -624,16 +600,16 @@
         scratch_shapes=[
             pltpu.VMEM((3, 2, 2, 1024), F32),
             pltpu.VMEM((2, 2, 1024), F32),
-            pltpu.VMEM(fixed[0].shape, F32),
+            pltpu.VMEM((96 + 128 + 56 + 24 + 8, 128), F32),
+            pltpu.VMEM(fixed[0].shape, BF16),
             pltpu.VMEM(fixed[1].shape, BF16),
             pltpu.VMEM(fixed[2].shape, BF16),
-            pltpu.VMEM(fixed[3].shape, BF16),
             pltpu.VMEM((16, 4, 8, 128), F32),
             pltpu.VMEM((9, 32, 128), F32),
             pltpu.VMEM((count_y, 32, 128), F32),
             pltpu.VMEM((count_x, 32, 128), F32),
             pltpu.VMEM((count_x, 16, 128), F32),
-            pltpu.VMEM((18, 8, 128), F32),
+            pltpu.VMEM((16, 18, 8, 128), F32),
             pltpu.VMEM((16, 10, 4, 32, 128), BF16),
             pltpu.VMEM((16, 3, 8, 128), F32),
             pltpu.VMEM((32, 64, 64), BF16),
@@ -644,19 +620,12 @@
             pltpu.VMEM((TILES * 128, 256), BF16),
             pltpu.VMEM((count_x // 4 * 128, 256), BF16),
             pltpu.VMEM((896, 256), F32),
-            pltpu.VMEM((1024, 128), BF16),
+            pltpu.VMEM((4, 1024, 128), BF16),
             pltpu.VMEM((64, 128), F32),
-            dma((6,)),
-            dma((16,)),
-            dma((16,)),
-            dma((8,)),
-            dma((8,)),
-            dma((count_y,)),
-            dma((count_y,)),
-            dma((6,)),
-            dma((6,)),
-            dma((count_x,)),
-            dma((count_x,)),
+            pltpu.VMEM((32, 64, 128), F32),
+            dma((5,)),
+            dma((5,)),
+            dma((5,)),
         ],
         compiler_params=pltpu.CompilerParams(
             collective_id=0, has_side_effects=True, vmem_limit_bytes=64 << 20

time: 37.4 us -> 34.9 us (0.933)
  Pallas kernels: 35.9 us -> 33.4 us
    pallas_call x1, Pallas kernels: 35.9 us -> 33.4 us  [body(): return call(offsets, charges, *fixed)]
where the time goes in v3:
time: 34.9 us; the launch traced here: 34.7 us
  Pallas kernels  33.4 us (96%)
  local copies, waits for them, and re-layouts  1.32 us (4%)
    pallas_call x1, Pallas kernels, body(): return call(offsets, charges, *fixed)  33.4 us
    unnamed x1, local copies, waits for them, and re-layouts  1.32 us

profile of v3, /device:TPU:1, one launch (start us, length us, event | category | flops | bytes accessed | tf_op | source)
XLA Modules:
  0.0 34.7 jit_solution(12006310235354792590)
XLA Ops:
  0.0 33.4 %shard_map.55 = f32[2,2,1024]{2,1,0:T(2,128)} custom-call(f32[3,2,2,1024]{3,2,1,0:T(2,128)} %off_hbm.1, f32[2,2,1024]{2,1,0:T(2,128)} %charge_hbm.1, bf16[256,256]{1,0:T(8,128)(2,1)} %constant.6.clone.uf_hbm, bf16[2,512,64]{2,1,0:T(8,128)(2,1)} %constant.7.clone.u2_hbm, bf16[4,256,64]{2,1,0:T(8,128)(2,1)} %constant.8.clone.dn_hbm), custom_call_target="tpu_custom_call" | custom-call | tf_op jit(solution)/shard_map/pallas_call | solution.py:636
  33.4 1.3 %copy.7 = f32[2,2,1024]{2,1,0:T(2,128)} copy(f32[2,2,1024]{2,1,0:T(2,128)} %shard_map.55) | data formatting | bytes 32768

commit v4 on v3

--- a/solution.py
+++ b/solution.py
@@ -14,6 +14,7 @@
 BF16 = jnp.bfloat16
 DIRS = [(ox, oy) for ox in (-1, 0, 1) for oy in (-1, 0, 1) if (ox, oy) != (0, 0)]
 ROWS = (1, 2, 3, -1, -2, -3)
+WIDER = (1, 2, 3, 4, 5, 6, 7, -1, -2, -3, -4, -5, -6, -7)
 TILES = 25
 
 
@@ -71,7 +72,7 @@
     off_hbm, charge_hbm, uf_hbm, u2_hbm, dn_hbm,
     out_ref,
     off_ref, charge_ref, flat, uf_ref, u2_ref, dn_ref,
-    halo, moments, near_rows, rows, coarse, pieces, source, charge, target, sums, near,
+    halo, moments, near_rows, rows, seconds, thirds, pieces, source, charge, target, sums, near,
     table, table3, right, right3, product, bq, leaf, bases,
     load_s, send_s, recv_s,
 ):
@@ -146,8 +147,7 @@
     for k in range(1, count_x):
         greet(k, 0)
 
-    @pl.loop(0, TILES)
-    def _(j):
+    def table_tile(j):
         dx = [(2 * j + e) // 7 - 3 for e in range(2)]
         dy = [(2 * j + e) % 7 - 3 for e in range(2)]
         dx, dy = (jnp.where(lane < 64, v[0], v[1]).astype(F32) for v in (dx, dy))
@@ -181,6 +181,8 @@
             table3[64 * i : 64 * i + 64, at] = hi
             table3[192 + 64 * i : 256 + 64 * i, at] = lo
 
+    pl.loop(0, 8)(table_tile)
+
     def basis(column, k):
         x = 2.0 * halo[column, 0, k : k + 1, :] - 1.0
         y = 2.0 * halo[column, 1, k : k + 1, :] - 1.0
@@ -210,6 +212,28 @@
                 for comp in range(3):
                     halo[column_of(cx, cy), comp, k : k + 1] = off_ref[comp, cx, cy : cy + 1, at]
                 halo[column_of(cx, cy), 3, k : k + 1] = charge_ref[cx, cy : cy + 1, at]
+    ROW, HALO, LEAF, LINE, SECOND, THIRD = range(6)
+    buffers = (near_rows, halo, moments, rows, seconds, thirds)
+    counts = (count_y - 1, 12, 8, 6, len(WIDER), count_x - 1)
+
+    def send(kind, index, at, dx, dy):
+        buffer = buffers[kind]
+        sems = (send_s.at[kind], recv_s.at[kind])
+        remote(buffer.at[index], buffer.at[at], *sems, dx, dy).start()
+
+    def all_of(kind):
+        part = buffers[kind].at[pl.ds(0, counts[kind])]
+        return remote(part, part, send_s.at[kind], recv_s.at[kind], 1, 1)
+
+    pl.semaphore_wait(barrier, len(DIRS) + count_y - 1 + count_x - 1)
+    for ox, oy in DIRS:
+        take_x = {1: [2], -1: [1], 0: [1, 2]}[ox]
+        put_x = {1: [0], -1: [3], 0: [1, 2]}[ox]
+        take_y = {1: (2, 1), -1: (1, 1), 0: (1, 2)}[oy]
+        put_y = {1: 0, -1: 3, 0: 1}[oy]
+        for a, b in zip(take_x, put_x):
+            at = (pl.ds(a * 4 + take_y[0], take_y[1]), pl.ds(b * 4 + put_y, take_y[1]))
+            send(HALO, *at, ox, oy)
     half_row = lax.broadcasted_iota(jnp.int32, (128, 128), 0) // 64
     half_lane = lax.broadcasted_iota(jnp.int32, (128, 128), 1)
     parity = (half_row == half_lane % 2).astype(F32).astype(BF16)
@@ -247,44 +271,29 @@
     first = folded(dot(uf_ref[...], wide(stacked)), 128)
     first = first[:64] + pltpu.roll(first[64:], 127, 1)
     first = jnp.where((lane64 < 16) & (lane64 % 2 == 0), first, 0.0)
-    first = first[:32] + pltpu.roll(first[32:], 1, 1)
-    near_rows[iy] = pltpu.roll(first, 16 * iy, 1)
-
-    pl.semaphore_wait(barrier, len(DIRS) + count_y - 1 + count_x - 1)
-
-    ROW, HALO, LEAF, LINE, COARSE = range(5)
-    buffers = (near_rows, halo, moments, rows, coarse)
-    counts = (count_y - 1, 12, 8, 6, count_x - 1)
-
-    def send(kind, index, at, dx, dy):
-        buffer = buffers[kind]
-        sems = (send_s.at[kind], recv_s.at[kind])
-        remote(buffer.at[index], buffer.at[at], *sems, dx, dy).start()
-
-    def all_of(kind):
-        part = buffers[kind].at[pl.ds(0, counts[kind])]
-        return remote(part, part, send_s.at[kind], recv_s.at[kind], 1, 1)
+    packet = first[:8]
+    for g in range(1, 8):
+        packet = packet + pltpu.roll(first[8 * g : 8 * g + 8], 16 * g, 1)
+    near_rows[iy] = packet
 
     for k in range(1, count_y):
         send(ROW, iy, iy, 0, k)
     for ox, oy in DIRS:
-        take_x = {1: [2], -1: [1], 0: [1, 2]}[ox]
-        put_x = {1: [0], -1: [3], 0: [1, 2]}[ox]
-        take_y = {1: (2, 1), -1: (1, 1), 0: (1, 2)}[oy]
-        put_y = {1: 0, -1: 3, 0: 1}[oy]
-        for a, b in zip(take_x, put_x):
-            at = (pl.ds(a * 4 + take_y[0], take_y[1]), pl.ds(b * 4 + put_y, take_y[1]))
-            send(HALO, *at, ox, oy)
-    for ox, oy in DIRS:
         send(LEAF, 4, (1 - ox) * 3 + 1 - oy, ox, oy)
 
+    pl.loop(8, TILES)(table_tile)
+
     all_of(ROW).wait_recv()
-    row = near_rows[0]
-    for k in range(1, count_y):
-        row = row + near_rows[k]
-    rows[ix] = row
-    full = jnp.concatenate([row, pltpu.roll(row, 127, 1)], 0)
-    full = jnp.where(lane64 % 2 == 0, full, 0.0)
+    packets = [near_rows[k] for k in range(count_y)]
+    full = []
+    for g in range(8):
+        tile = jnp.zeros((8, 128), F32)
+        for k in range(count_y):
+            moved = pltpu.roll(packets[k], 16 * (k - g) % 128, 1) if k != g else packets[k]
+            tile = jnp.where(lane // 16 == k, moved, tile)
+        full.append(tile)
+    full = jnp.concatenate(full, 0)
+    rows[ix] = full[:32] + pltpu.roll(full[32:], 1, 1)
 
     def part(source, which, step_z, step_y):
         o = folded(dot(u2_ref[which], wide(source)), 256)
@@ -299,16 +308,24 @@
     second = jnp.where((lane64 // 16 % 2 == 0) & (lane64 % 4 == 0), second, 0.0)
     third = part(second, ix // 2 % 2, 4, 32)
     third = jnp.where((lane64 // 16 % 4 == 0) & (lane64 % 8 == 0), third, 0.0)
-    packed = second[:16] + pltpu.roll(third[:16], 16, 1)
-    for g in range(1, 4):
-        at = slice(16 * g, 16 * g + 16)
-        packed = packed + pltpu.roll(second[at], g, 1) + pltpu.roll(third[at], 16 + g, 1)
-    coarse[ix] = packed
-
-    for k in range(1, count_x):
-        send(COARSE, ix, ix, k, 0)
+    packed = second[:8]
+    for g in range(1, 8):
+        packed = packed + pltpu.roll(second[8 * g : 8 * g + 8], g % 4 + 16 * (g // 4), 1)
+    seconds[ix] = packed
+    packed = third[:8]
+    for g in range(1, 8):
+        packed = packed + pltpu.roll(third[8 * g : 8 * g + 8], g, 1)
+    pair = packed[:2]
+    for e in range(1, 4):
+        pair = pair + pltpu.roll(packed[2 * e : 2 * e + 2], 16 * e, 1)
+    thirds[ix] = pair
+
     for dx in ROWS:
         send(LINE, ix, ix, dx, 0)
+    for dx in WIDER:
+        send(SECOND, ix, ix, dx, 0)
+    for k in range(1, count_x):
+        send(THIRD, ix, ix, k, 0)
 
     first_term = (sub == 0) | (sub == 1) | (sub == 3)
     second_term = (sub == 2) | (sub == 4)
@@ -451,17 +468,14 @@
             mine = jnp.where(eye, value[64 * k : 64 * k + 64], 0.0)
             near[col, k : k + 1] = jnp.sum(mine, 0, keepdims=True)
 
-    for kind in (LEAF, LINE, COARSE):
+    for kind in (LEAF, LINE, SECOND, THIRD):
         all_of(kind).wait_recv()
 
-    def unpacked(value, start):
-        return jnp.concatenate(
-            [pltpu.roll(value, lax.rem(start - g + 128, 128), 1) for g in range(4)], 0
-        )
-
     for j in range(count_x // 4):
-        group = coarse[4 * j] + coarse[4 * j + 1] + coarse[4 * j + 2] + coarse[4 * j + 3]
-        third = unpacked(group, jnp.int32(112))
+        group = thirds[4 * j] + thirds[4 * j + 1] + thirds[4 * j + 2] + thirds[4 * j + 3]
+        group = jnp.concatenate([group] + [pltpu.roll(group, 128 - 16 * e, 1) for e in range(1, 4)], 0)
+        third = [group] + [pltpu.roll(group, 128 - g, 1) for g in range(1, 8)]
+        third = jnp.concatenate(third, 0)
         right3[128 * j : 128 * j + 64] = wide(third)
         right3[128 * j + 64 : 128 * j + 128] = wide(pltpu.roll(third, 64, 1))
     o = folded(dot(table3[...], right3[...]), 192)
@@ -523,7 +537,10 @@
         line = line * within(ix + dx, count_x, dx, ix % 2)
         x2 = ix // 2 + dx
         base = lax.rem(2 * x2 + 2 * count_x, count_x)
-        pair = unpacked(coarse[base] + coarse[base + 1], lax.rem(80 - 32 * (iy // 2) + 128, 128))
+        pair = seconds[base] + seconds[base + 1]
+        pair = pltpu.roll(pair, lax.rem(80 - 32 * (iy // 2) + 128, 128), 1)
+        pair = [pltpu.roll(pair, (-(g % 4) - 16 * (g // 4)) % 128, 1) if g else pair for g in range(8)]
+        pair = jnp.concatenate(pair, 0)
         pair = pair * within(x2, count_x // 2, dx, ix // 2 % 2)
         for dy in range(-3, 4):
             one = pltpu.roll(line, (-16 * dy) % 128, 1) * within(iy + dy, count_y, dy, iy % 2)
@@ -582,7 +599,7 @@
             at = slice(128 * k, 128 * k + 128)
             out_ref[col // 2, col % 2 : col % 2 + 1, at] = near[col, k : k + 1]
 
-    for kind in range(5):
+    for kind in range(6):
         all_of(kind).wait_send()
 
 
@@ -606,9 +623,10 @@
             pltpu.VMEM(fixed[2].shape, BF16),
             pltpu.VMEM((16, 4, 8, 128), F32),
             pltpu.VMEM((9, 32, 128), F32),
-            pltpu.VMEM((count_y, 32, 128), F32),
+            pltpu.VMEM((count_y, 8, 128), F32),
             pltpu.VMEM((count_x, 32, 128), F32),
-            pltpu.VMEM((count_x, 16, 128), F32),
+            pltpu.VMEM((count_x, 8, 128), F32),
+            pltpu.VMEM((count_x, 2, 128), F32),
             pltpu.VMEM((16, 18, 8, 128), F32),
             pltpu.VMEM((16, 10, 4, 32, 128), BF16),
             pltpu.VMEM((16, 3, 8, 128), F32),
@@ -624,8 +642,8 @@
             pltpu.VMEM((64, 128), F32),
             pltpu.VMEM((32, 64, 128), F32),
             dma((5,)),
-            dma((5,)),
-            dma((5,)),
+            dma((6,)),
+            dma((6,)),
         ],
         compiler_params=pltpu.CompilerParams(
             collective_id=0, has_side_effects=True, vmem_limit_bytes=64 << 20

time: 34.9 us -> 31.9 us (0.914)
  Pallas kernels: 33.4 us -> 30.4 us
    pallas_call x1, Pallas kernels: 33.4 us -> 30.4 us  [body(): return call(offsets, charges, *fixed)]
where the time goes in v4:
time: 31.9 us; the launch traced here: 31.7 us
  Pallas kernels  30.4 us (95%)
  local copies, waits for them, and re-layouts  1.32 us (4%)
    pallas_call x1, Pallas kernels, body(): return call(offsets, charges, *fixed)  30.4 us
    unnamed x1, local copies, waits for them, and re-layouts  1.32 us

profile of v4, /device:TPU:1, one launch (start us, length us, event | category | flops | bytes accessed | tf_op | source)
XLA Modules:
  0.0 31.7 jit_solution(2066682118317408749)
XLA Ops:
  0.0 30.4 %shard_map.55 = f32[2,2,1024]{2,1,0:T(2,128)} custom-call(f32[3,2,2,1024]{3,2,1,0:T(2,128)} %off_hbm.1, f32[2,2,1024]{2,1,0:T(2,128)} %charge_hbm.1, bf16[256,256]{1,0:T(8,128)(2,1)} %constant.6.clone.uf_hbm, bf16[2,512,64]{2,1,0:T(8,128)(2,1)} %constant.7.clone.u2_hbm, bf16[4,256,64]{2,1,0:T(8,128)(2,1)} %constant.8.clone.dn_hbm), custom_call_target="tpu_custom_call" | custom-call | tf_op jit(solution)/shard_map/pallas_call | solution.py:654
  30.4 1.3 %copy.7 = f32[2,2,1024]{2,1,0:T(2,128)} copy(f32[2,2,1024]{2,1,0:T(2,128)} %shard_map.55) | data formatting | bytes 32768

commit v5 on v4

--- a/solution.py
+++ b/solution.py
@@ -44,9 +44,7 @@
     uf = np.concatenate(split(uf), 0)
     u2 = up.transpose(0, 1, 2, 4, 3).reshape(2, 256, 64)
     u2 = np.concatenate(split(u2), 1)
-    dn = up.reshape(4, 128, 64)
-    dn = np.concatenate(split(dn), 1)
-    return [uf, u2, dn]
+    return [uf, u2]
 
 
 def pair_split(x):
@@ -69,9 +67,9 @@
 
 def kernel(
     count_x, count_y,
-    off_hbm, charge_hbm, uf_hbm, u2_hbm, dn_hbm,
+    off_hbm, charge_hbm, uf_hbm, u2_hbm,
     out_ref,
-    off_ref, charge_ref, flat, uf_ref, u2_ref, dn_ref,
+    off_ref, charge_ref, flat, uf_ref, u2_ref,
     halo, moments, near_rows, rows, seconds, thirds, pieces, source, charge, target, sums, near,
     table, table3, right, right3, product, bq, leaf, bases,
     load_s, send_s, recv_s,
@@ -80,7 +78,7 @@
         pltpu.make_async_copy(src, dst, load_s.at[i])
         for i, (src, dst) in enumerate(
             [(off_hbm, off_ref), (charge_hbm, charge_ref)]
-            + [(uf_hbm, uf_ref), (u2_hbm, u2_ref), (dn_hbm, dn_ref)]
+            + [(uf_hbm, uf_ref), (u2_hbm, u2_ref)]
         )
     ]
     for load in loads:
@@ -114,7 +112,7 @@
     for i in range(7):
         gap = gap_z + (i - 3.0)
         flat[at_z2 + 8 * i : at_z2 + 8 * i + 8] = gap * gap
-    for level, start, length in ((0, 0, 64), (1, 64, 16), (2, 80, 16)):
+    for level, start, length in ((0, 0, 64), (1, 0, 16), (2, 16, 16)):
         z = lane % 16
         seen = z + (sub - 3) * 2**level
         odd = (z // 2**level) % 2
@@ -183,10 +181,17 @@
 
     pl.loop(0, 8)(table_tile)
 
-    def basis(column, k):
-        x = 2.0 * halo[column, 0, k : k + 1, :] - 1.0
-        y = 2.0 * halo[column, 1, k : k + 1, :] - 1.0
-        z = 2.0 * halo[column, 2, k : k + 1, :] - 1.0
+    def basis(column, k, level=0, col=None):
+        places = [halo[column, comp, k : k + 1, :] for comp in range(3)]
+        if level:
+            size = 2**level
+            corner = (
+                ((2 * ix + col // 2) % size).astype(F32),
+                ((2 * iy + col % 2) % size).astype(F32),
+                (2 * k) % size + (lane[:1] // 64).astype(F32),
+            )
+            places = [(place + at) * (1.0 / size) for place, at in zip(places, corner)]
+        x, y, z = (2.0 * place - 1.0 for place in places)
 
         def poly(i, u):
             p = [flat[32 * i + 8 * e : 32 * i + 8 * e + 8] for e in range(4)]
@@ -245,7 +250,7 @@
         column = (1 + col // 2) * 4 + 1 + col % 2
         for k in range(8):
             value = basis(column, k)
-            bases[8 * col + k] = value
+            bases[0, 8 * col + k] = value
             value = value * halo[column, 3, k : k + 1, :]
             hi, lo = pair_split(value)
             bq[col, 64 * k : 64 * k + 64] = hi
@@ -283,49 +288,12 @@
 
     pl.loop(8, TILES)(table_tile)
 
-    all_of(ROW).wait_recv()
-    packets = [near_rows[k] for k in range(count_y)]
-    full = []
-    for g in range(8):
-        tile = jnp.zeros((8, 128), F32)
-        for k in range(count_y):
-            moved = pltpu.roll(packets[k], 16 * (k - g) % 128, 1) if k != g else packets[k]
-            tile = jnp.where(lane // 16 == k, moved, tile)
-        full.append(tile)
-    full = jnp.concatenate(full, 0)
-    rows[ix] = full[:32] + pltpu.roll(full[32:], 1, 1)
-
-    def part(source, which, step_z, step_y):
-        o = folded(dot(u2_ref[which], wide(source)), 256)
-        return (
-            o[:64]
-            + pltpu.roll(o[64:128], 128 - step_z, 1)
-            + pltpu.roll(o[128:192], 128 - step_y, 1)
-            + pltpu.roll(o[192:], 128 - step_z - step_y, 1)
-        )
-
-    second = part(full, ix % 2, 2, 16)
-    second = jnp.where((lane64 // 16 % 2 == 0) & (lane64 % 4 == 0), second, 0.0)
-    third = part(second, ix // 2 % 2, 4, 32)
-    third = jnp.where((lane64 // 16 % 4 == 0) & (lane64 % 8 == 0), third, 0.0)
-    packed = second[:8]
-    for g in range(1, 8):
-        packed = packed + pltpu.roll(second[8 * g : 8 * g + 8], g % 4 + 16 * (g // 4), 1)
-    seconds[ix] = packed
-    packed = third[:8]
-    for g in range(1, 8):
-        packed = packed + pltpu.roll(third[8 * g : 8 * g + 8], g, 1)
-    pair = packed[:2]
-    for e in range(1, 4):
-        pair = pair + pltpu.roll(packed[2 * e : 2 * e + 2], 16 * e, 1)
-    thirds[ix] = pair
-
-    for dx in ROWS:
-        send(LINE, ix, ix, dx, 0)
-    for dx in WIDER:
-        send(SECOND, ix, ix, dx, 0)
-    for k in range(1, count_x):
-        send(THIRD, ix, ix, k, 0)
+    @pl.loop(0, 4, unroll=True)
+    def _(col):
+        column = (1 + col // 2) * 4 + 1 + col % 2
+        for level in range(1, 4):
+            for k in range(8):
+                bases[level, 8 * col + k] = basis(column, k, level, col)
 
     first_term = (sub == 0) | (sub == 1) | (sub == 3)
     second_term = (sub == 2) | (sub == 4)
@@ -385,16 +353,13 @@
             target[col * 8 + k] = stack[:64]
             target[col * 8 + k + 1] = stack[64:]
 
-    all_of(HALO).wait_recv()
-
     outside = jnp.where(lax.broadcasted_iota(jnp.int32, (32, 128), 0) == 6, 16384.0, 0.0)
     lane32 = lane64[:32] < 64
     left_half = lane32
     outside_low = jnp.where(left_half, outside, 0.0).astype(BF16)
     outside_high = jnp.where(left_half, 0.0, outside).astype(BF16)
 
-    @pl.loop(0, 16, unroll=4)
-    def _(column):
+    def source_column(column):
         wx, wy = column // 4, column % 4
         features(column, wx.astype(F32) - 1.0, wy.astype(F32) - 1.0, True)
         at_x, at_y = 2 * ix + wx - 1, 2 * iy + wy - 1
@@ -425,13 +390,9 @@
                 source[column, k + 1, 2 * e] = jnp.where(left_half, tiles, 0.0).astype(BF16)
                 source[column, k + 1, 2 * e + 1] = jnp.where(left_half, 0.0, tiles).astype(BF16)
 
-    def near_block(block, carry):
-        col, k = block // 8, block % 8
-        cx, cy = col // 2, col % 2
-        mine = target[block]
+    def near_sum(mine, k, columns, own):
         straight = jnp.zeros((64, 128), F32)
         crossed = jnp.zeros((64, 128), F32)
-        columns = [(cx + dx) * 4 + cy + dy for dx in range(3) for dy in range(3)]
 
         def side(column, a, b):
             return jnp.concatenate([source[column, a[0], a[1]], source[column, b[0], b[1]]], 0)
@@ -445,19 +406,95 @@
             inverse = lax.rsqrt(dot(mine, jnp.concatenate([above, below], 1)))
             crossed = crossed + inverse[:, :128] * row_of(column, 2)
             crossed = crossed + inverse[:, 128:] * row_of(column, 0)
-        for i in range(0, 9, 2):
+        for i in range(0, len(columns), 2):
             group = columns[i : i + 2]
             both = [side(column, (k + 1, 0), (k + 1, 1)) for column in group]
             inverse = lax.rsqrt(dot(mine, jnp.concatenate(both, 1)))
             for e, column in enumerate(group):
                 value = inverse[:, 128 * e : 128 * e + 128]
-                if i + e == 4:
+                if own and i + e == 0:
                     value = jnp.where(eye, 0.0, value)
                 straight = straight + value * row_of(column, 1)
-        sums[block] = straight + pltpu.roll(crossed, 64, 1)
+        return straight + pltpu.roll(crossed, 64, 1)
+
+    @pl.loop(0, 4, unroll=True)
+    def _(col):
+        source_column((1 + col // 2) * 4 + 1 + col % 2)
+
+    def inner_block(block, carry):
+        col, k = block // 8, block % 8
+        cx, cy = col // 2, col % 2
+        columns = [(1 + a) * 4 + 1 + b for a in (cx, 1 - cx) for b in (cy, 1 - cy)]
+        sums[block] = near_sum(target[block], k, columns, True)
         return carry
 
-    lax.fori_loop(0, 32, near_block, 0, unroll=8)
+    lax.fori_loop(0, 32, inner_block, 0, unroll=8)
+
+    all_of(ROW).wait_recv()
+    packets = [near_rows[k] for k in range(count_y)]
+    full = []
+    for g in range(8):
+        tile = jnp.zeros((8, 128), F32)
+        for k in range(count_y):
+            moved = pltpu.roll(packets[k], 16 * (k - g) % 128, 1) if k != g else packets[k]
+            tile = jnp.where(lane // 16 == k, moved, tile)
+        full.append(tile)
+    full = jnp.concatenate(full, 0)
+    rows[ix] = full[:32] + pltpu.roll(full[32:], 1, 1)
+
+    def part(source, which, step_z, step_y):
+        o = folded(dot(u2_ref[which], wide(source)), 256)
+        return (
+            o[:64]
+            + pltpu.roll(o[64:128], 128 - step_z, 1)
+            + pltpu.roll(o[128:192], 128 - step_y, 1)
+            + pltpu.roll(o[192:], 128 - step_z - step_y, 1)
+        )
+
+    second = part(full, ix % 2, 2, 16)
+    second = jnp.where((lane64 // 16 % 2 == 0) & (lane64 % 4 == 0), second, 0.0)
+    third = part(second, ix // 2 % 2, 4, 32)
+    third = jnp.where((lane64 // 16 % 4 == 0) & (lane64 % 8 == 0), third, 0.0)
+    packed = second[:8]
+    for g in range(1, 8):
+        packed = packed + pltpu.roll(second[8 * g : 8 * g + 8], g % 4 + 16 * (g // 4), 1)
+    seconds[ix] = packed
+    packed = third[:8]
+    for g in range(1, 8):
+        packed = packed + pltpu.roll(third[8 * g : 8 * g + 8], g, 1)
+    pair = packed[:2]
+    for e in range(1, 4):
+        pair = pair + pltpu.roll(packed[2 * e : 2 * e + 2], 16 * e, 1)
+    thirds[ix] = pair
+
+    for dx in ROWS:
+        send(LINE, ix, ix, dx, 0)
+    for dx in WIDER:
+        send(SECOND, ix, ix, dx, 0)
+    for k in range(1, count_x):
+        send(THIRD, ix, ix, k, 0)
+
+    all_of(HALO).wait_recv()
+
+
+    @pl.loop(0, 4, unroll=True)
+    def _(e):
+        for column in (e, 12 + e):
+            source_column(column)
+
+    @pl.loop(0, 2, unroll=True)
+    def _(e):
+        for column in (4, 7):
+            source_column(column + 4 * e)
+
+    def outer_block(block, carry):
+        col, k = block // 8, block % 8
+        cx, cy = col // 2, col % 2
+        columns = [12 * cx + cy + b for b in range(3)] + [4 + 3 * cy, 8 + 3 * cy]
+        sums[block] = sums[block] + near_sum(target[block], k, columns, False)
+        return carry
+
+    lax.fori_loop(0, 32, outer_block, 0, unroll=8)
 
     @pl.loop(0, 4, unroll=True)
     def _(col):
@@ -468,23 +505,8 @@
             mine = jnp.where(eye, value[64 * k : 64 * k + 64], 0.0)
             near[col, k : k + 1] = jnp.sum(mine, 0, keepdims=True)
 
-    for kind in (LEAF, LINE, SECOND, THIRD):
-        all_of(kind).wait_recv()
-
-    for j in range(count_x // 4):
-        group = thirds[4 * j] + thirds[4 * j + 1] + thirds[4 * j + 2] + thirds[4 * j + 3]
-        group = jnp.concatenate([group] + [pltpu.roll(group, 128 - 16 * e, 1) for e in range(1, 4)], 0)
-        third = [group] + [pltpu.roll(group, 128 - g, 1) for g in range(1, 8)]
-        third = jnp.concatenate(third, 0)
-        right3[128 * j : 128 * j + 64] = wide(third)
-        right3[128 * j + 64 : 128 * j + 128] = wide(pltpu.roll(third, 64, 1))
-    o = folded(dot(table3[...], right3[...]), 192)
-    local = o[64:128]
-    local = local + jnp.where(lane64 == 0, pltpu.roll(o[128:], 120, 1), 0.0)
-    local = local + jnp.where(lane64 == 8, pltpu.roll(o[:64], 8, 1), 0.0)
-    local3 = jnp.where((lane64 < 16) & (lane64 % 8 == 0), 0.125 * local, 0.0)
-
-    plain, crossed = {}, {}
+    all_of(LEAF).wait_recv()
+    plain = {}
     for ox in (-1, 0, 1):
         for oy in (-1, 0, 1):
             value = moments[(ox + 1) * 3 + oy + 1]
@@ -522,6 +544,44 @@
                 result = value if result is None else result + value
         return result
 
+    for dx in range(-3, 4):
+        for dy in range(-3, 4):
+            value = leaf_block(dx, dy)
+            high = value.astype(BF16).astype(F32)
+            at = ((dx + 3) * 7 + dy + 3) * 64
+            right[at : at + 64] = jnp.where(lane64 < 64, high, value - high).astype(BF16)
+    right[49 * 64 : 50 * 64] = jnp.zeros((64, 128), BF16)
+
+    product[...] = dot(table[...], right[...])
+
+    def shifted(i, fold, levels):
+        o = product[64 * i : 64 * i + 64] + product[448 + 64 * i : 512 + 64 * i]
+        o = o + pltpu.roll(o, fold, 1)
+        total = jnp.zeros((64, 128), F32)
+        for level in levels:
+            value = o if i == 3 else pltpu.roll(o, (-(i - 3) * 2**level) % 128, 1)
+            total = total + value * flat[at_w + 8 * level + i : at_w + 8 * level + i + 1]
+        return total
+
+    far = shifted(0, 64, (0,))
+    for i in range(1, 7):
+        far = far + shifted(i, 64, (0,))
+    leaf[...] = far
+
+    @pl.loop(0, 4, unroll=True)
+    def _(col):
+        here = pltpu.roll(leaf[...], (128 - 16 * col) % 128, 1)
+        for k in range(8):
+            spread = jnp.where(
+                lane64 < 64,
+                jnp.broadcast_to(here[:, 2 * k : 2 * k + 1], (64, 128)),
+                jnp.broadcast_to(here[:, 2 * k + 1 : 2 * k + 2], (64, 128)),
+            )
+            both = jnp.sum(bases[0, 8 * col + k] * spread, 0, keepdims=True)
+            near[col, k : k + 1] = near[col, k : k + 1] + both
+
+    for kind in (LINE, SECOND):
+        all_of(kind).wait_recv()
     def within(value, count, step, odd):
         ok = (value >= 0) & (value < count)
         if step == 3:
@@ -533,12 +593,12 @@
     for dx in range(-3, 4):
         line = rows[lax.rem(ix + dx + count_x, count_x)]
         line = jnp.concatenate([line, pltpu.roll(line, 127, 1)], 0)
-        line = pltpu.roll(line, lax.rem(64 - 16 * iy + 128, 128), 1)
+        line = pltpu.roll(line, lax.rem(128 - 16 * iy, 128), 1)
         line = line * within(ix + dx, count_x, dx, ix % 2)
         x2 = ix // 2 + dx
         base = lax.rem(2 * x2 + 2 * count_x, count_x)
         pair = seconds[base] + seconds[base + 1]
-        pair = pltpu.roll(pair, lax.rem(80 - 32 * (iy // 2) + 128, 128), 1)
+        pair = pltpu.roll(pair, lax.rem(144 - 32 * (iy // 2), 128), 1)
         pair = [pltpu.roll(pair, (-(g % 4) - 16 * (g // 4)) % 128, 1) if g else pair for g in range(8)]
         pair = jnp.concatenate(pair, 0)
         pair = pair * within(x2, count_x // 2, dx, ix // 2 % 2)
@@ -546,58 +606,46 @@
             one = pltpu.roll(line, (-16 * dy) % 128, 1) * within(iy + dy, count_y, dy, iy % 2)
             two = pltpu.roll(pair, (-32 * dy) % 128, 1)
             two = two * within(iy // 2 + dy, count_y // 2, dy, iy // 2 % 2)
-            value = jnp.where(lane64 < 64, leaf_block(dx, dy), jnp.where(lane64 < 80, one, two))
-            value = jnp.where(lane64 < 96, value, 0.0)
+            value = jnp.where(lane64 < 16, one, two)
+            high = value.astype(BF16).astype(F32)
+            low = jnp.where(lane64 < 64, pltpu.roll(value - high, 32, 1), 0.0)
             at = ((dx + 3) * 7 + dy + 3) * 64
-            right[at : at + 64] = wide(value)
-    right[49 * 64 : 50 * 64] = jnp.zeros((64, 256), BF16)
+            right[at : at + 64] = jnp.where(lane64 < 32, high, low).astype(BF16)
 
     product[...] = dot(table[...], right[...])
 
-    far = jnp.zeros((64, 128), F32)
-    for i in range(7):
-        dz = i - 3
-        o = product[64 * i : 64 * i + 64]
-        o2 = product[448 + 64 * i : 512 + 64 * i]
-        o = o[:, :128] + o[:, 128:] + o2[:, :128] + o2[:, 128:]
-        for level in range(3):
-            value = o if dz == 0 else pltpu.roll(o, (-dz * 2**level) % 128, 1)
-            far = far + value * flat[at_w + 8 * level + i : at_w + 8 * level + i + 1]
-
-    def down(source, which, step):
-        o = folded(dot(dn_ref[which], wide(source)), 128)
-        return jnp.where(lane64 % (2 * step) == 0, o[:64], pltpu.roll(o[64:], step, 1))
-
-    low = lane64 < 16
-    local2 = down(local3, ix // 2 % 2 * 2 + iy // 2 % 2, 4) + pltpu.roll(far, 48, 1)
-    local2 = jnp.where(low & (lane64 % 4 == 0), local2, 0.0)
-    local1 = down(local2, ix % 2 * 2 + iy % 2, 2) + pltpu.roll(far, 64, 1)
-    local1 = jnp.where(low & (lane64 % 2 == 0), local1, 0.0)
-    local0 = far
-    for col in range(4):
-        value = down(local1, col, 1)
-        if col:
-            value = pltpu.roll(value, 16 * col, 1)
-        local0 = local0 + jnp.where(lane64 // 16 == col, value, 0.0)
-    leaf[...] = local0
-
-    @pl.loop(0, 4, unroll=True)
-    def _(col):
-        column = (1 + col // 2) * 4 + 1 + col % 2
-        here = pltpu.roll(leaf[...], lax.rem(128 - 16 * col, 128), 1)
-        for k in range(8):
-            spread = jnp.where(
-                lane64 < 64,
-                jnp.broadcast_to(here[:, 2 * k : 2 * k + 1], (64, 128)),
-                jnp.broadcast_to(here[:, 2 * k + 1 : 2 * k + 2], (64, 128)),
-            )
-            both = bases[8 * col + k] * spread
-            near[col, k : k + 1] = jnp.sum(both, 0, keepdims=True) + near[col, k : k + 1]
-
-    for col in range(4):
-        for k in range(8):
-            at = slice(128 * k, 128 * k + 128)
-            out_ref[col // 2, col % 2 : col % 2 + 1, at] = near[col, k : k + 1]
+    far12 = shifted(0, 96, (1, 2))
+    for i in range(1, 7):
+        far12 = far12 + shifted(i, 96, (1, 2))
+
+    all_of(THIRD).wait_recv()
+    for j in range(count_x // 4):
+        group = thirds[4 * j] + thirds[4 * j + 1] + thirds[4 * j + 2] + thirds[4 * j + 3]
+        group = jnp.concatenate([group] + [pltpu.roll(group, 128 - 16 * e, 1) for e in range(1, 4)], 0)
+        third = [group] + [pltpu.roll(group, 128 - g, 1) for g in range(1, 8)]
+        third = jnp.concatenate(third, 0)
+        right3[128 * j : 128 * j + 64] = wide(third)
+        right3[128 * j + 64 : 128 * j + 128] = wide(pltpu.roll(third, 64, 1))
+    o = folded(dot(table3[...], right3[...]), 192)
+    local = o[64:128]
+    local = local + jnp.where(lane64 == 0, pltpu.roll(o[128:], 120, 1), 0.0)
+    local = local + jnp.where(lane64 == 8, pltpu.roll(o[:64], 8, 1), 0.0)
+    local3 = jnp.where((lane64 < 16) & (lane64 % 8 == 0), 0.125 * local, 0.0)
+
+    def column(value, at):
+        return jnp.broadcast_to(value[:, at : at + 1], (64, 128))
+
+    for k in range(8):
+        if k % 4 == 0:
+            high3 = column(local3, 2 * k)
+        if k % 2 == 0:
+            high2 = column(far12, 16 + 2 * k)
+        high1 = column(far12, 2 * k)
+        for col in range(4):
+            block = 8 * col + k
+            both = bases[1, block] * high1 + bases[2, block] * high2 + bases[3, block] * high3
+            both = jnp.sum(both, 0, keepdims=True) + near[col, k : k + 1]
+            out_ref[col // 2, col % 2 : col % 2 + 1, 128 * k : 128 * k + 128] = both
 
     for kind in range(6):
         all_of(kind).wait_send()
@@ -620,7 +668,6 @@
             pltpu.VMEM((96 + 128 + 56 + 24 + 8, 128), F32),
             pltpu.VMEM(fixed[0].shape, BF16),
             pltpu.VMEM(fixed[1].shape, BF16),
-            pltpu.VMEM(fixed[2].shape, BF16),
             pltpu.VMEM((16, 4, 8, 128), F32),
             pltpu.VMEM((9, 32, 128), F32),
             pltpu.VMEM((count_y, 8, 128), F32),
@@ -635,13 +682,13 @@
             pltpu.VMEM((4, 8, 128), F32),
             pltpu.VMEM((896, TILES * 128), BF16),
             pltpu.VMEM((384, count_x // 4 * 128), BF16),
-            pltpu.VMEM((TILES * 128, 256), BF16),
+            pltpu.VMEM((TILES * 128, 128), BF16),
             pltpu.VMEM((count_x // 4 * 128, 256), BF16),
-            pltpu.VMEM((896, 256), F32),
+            pltpu.VMEM((896, 128), F32),
             pltpu.VMEM((4, 1024, 128), BF16),
             pltpu.VMEM((64, 128), F32),
-            pltpu.VMEM((32, 64, 128), F32),
-            dma((5,)),
+            pltpu.VMEM((4, 32, 64, 128), F32),
+            dma((4,)),
             dma((6,)),
             dma((6,)),
         ],

time: 31.9 us -> 33.8 us (1.060)
  Pallas kernels: 30.4 us -> 32.3 us
    pallas_call x1, Pallas kernels: 30.4 us -> 32.3 us  [body(): return call(offsets, charges, *fixed)]
where the time goes in v5:
time: 33.8 us; the launch traced here: 33.7 us
  Pallas kernels  32.3 us (96%)
  local copies, waits for them, and re-layouts  1.32 us (4%)
    pallas_call x1, Pallas kernels, body(): return call(offsets, charges, *fixed)  32.3 us
    unnamed x1, local copies, waits for them, and re-layouts  1.32 us

profile of v5, /device:TPU:1, one launch (start us, length us, event | category | flops | bytes accessed | tf_op | source)
XLA Modules:
  0.0 33.7 jit_solution(4711077771859350020)
XLA Ops:
  0.0 32.3 %shard_map.46 = f32[2,2,1024]{2,1,0:T(2,128)} custom-call(f32[3,2,2,1024]{3,2,1,0:T(2,128)} %off_hbm.1, f32[2,2,1024]{2,1,0:T(2,128)} %charge_hbm.1, bf16[256,256]{1,0:T(8,128)(2,1)} %constant.4.clone.uf_hbm, bf16[2,512,64]{2,1,0:T(8,128)(2,1)} %constant.5.clone.u2_hbm), custom_call_target="tpu_custom_call" | custom-call | tf_op jit(solution)/shard_map/pallas_call | solution.py:701
  32.3 1.3 %copy.6 = f32[2,2,1024]{2,1,0:T(2,128)} copy(f32[2,2,1024]{2,1,0:T(2,128)} %shard_map.46) | data formatting | bytes 32768

commit v6 on v5

--- a/solution.py
+++ b/solution.py
@@ -13,7 +13,7 @@
 F32 = jnp.float32
 BF16 = jnp.bfloat16
 DIRS = [(ox, oy) for ox in (-1, 0, 1) for oy in (-1, 0, 1) if (ox, oy) != (0, 0)]
-ROWS = (1, 2, 3, -1, -2, -3)
+ROWS = (1, 2, -1, -2)
 WIDER = (1, 2, 3, 4, 5, 6, 7, -1, -2, -3, -4, -5, -6, -7)
 TILES = 25
 
@@ -219,7 +219,7 @@
                 halo[column_of(cx, cy), 3, k : k + 1] = charge_ref[cx, cy : cy + 1, at]
     ROW, HALO, LEAF, LINE, SECOND, THIRD = range(6)
     buffers = (near_rows, halo, moments, rows, seconds, thirds)
-    counts = (count_y - 1, 12, 8, 6, len(WIDER), count_x - 1)
+    counts = (count_y - 1, 12, 8, len(ROWS) + 1, len(WIDER), count_x - 1)
 
     def send(kind, index, at, dx, dy):
         buffer = buffers[kind]
@@ -230,15 +230,6 @@
         part = buffers[kind].at[pl.ds(0, counts[kind])]
         return remote(part, part, send_s.at[kind], recv_s.at[kind], 1, 1)
 
-    pl.semaphore_wait(barrier, len(DIRS) + count_y - 1 + count_x - 1)
-    for ox, oy in DIRS:
-        take_x = {1: [2], -1: [1], 0: [1, 2]}[ox]
-        put_x = {1: [0], -1: [3], 0: [1, 2]}[ox]
-        take_y = {1: (2, 1), -1: (1, 1), 0: (1, 2)}[oy]
-        put_y = {1: 0, -1: 3, 0: 1}[oy]
-        for a, b in zip(take_x, put_x):
-            at = (pl.ds(a * 4 + take_y[0], take_y[1]), pl.ds(b * 4 + put_y, take_y[1]))
-            send(HALO, *at, ox, oy)
     half_row = lax.broadcasted_iota(jnp.int32, (128, 128), 0) // 64
     half_lane = lax.broadcasted_iota(jnp.int32, (128, 128), 1)
     parity = (half_row == half_lane % 2).astype(F32).astype(BF16)
@@ -281,8 +272,17 @@
         packet = packet + pltpu.roll(first[8 * g : 8 * g + 8], 16 * g, 1)
     near_rows[iy] = packet
 
+    pl.semaphore_wait(barrier, len(DIRS) + count_y - 1 + count_x - 1)
     for k in range(1, count_y):
         send(ROW, iy, iy, 0, k)
+    for ox, oy in DIRS:
+        take_x = {1: [2], -1: [1], 0: [1, 2]}[ox]
+        put_x = {1: [0], -1: [3], 0: [1, 2]}[ox]
+        take_y = {1: (2, 1), -1: (1, 1), 0: (1, 2)}[oy]
+        put_y = {1: 0, -1: 3, 0: 1}[oy]
+        for a, b in zip(take_x, put_x):
+            at = (pl.ds(a * 4 + take_y[0], take_y[1]), pl.ds(b * 4 + put_y, take_y[1]))
+            send(HALO, *at, ox, oy)
     for ox, oy in DIRS:
         send(LEAF, 4, (1 - ox) * 3 + 1 - oy, ox, oy)
 
@@ -428,7 +428,7 @@
         sums[block] = near_sum(target[block], k, columns, True)
         return carry
 
-    lax.fori_loop(0, 32, inner_block, 0, unroll=8)
+    lax.fori_loop(0, 32, inner_block, 0, unroll=16)
 
     all_of(ROW).wait_recv()
     packets = [near_rows[k] for k in range(count_y)]
@@ -467,12 +467,13 @@
         pair = pair + pltpu.roll(packed[2 * e : 2 * e + 2], 16 * e, 1)
     thirds[ix] = pair
 
+    for k in range(1, count_x):
+        send(THIRD, ix, ix, k, 0)
+    for dx in WIDER:
+        send(SECOND, ix, ix, dx, 0)
     for dx in ROWS:
         send(LINE, ix, ix, dx, 0)
-    for dx in WIDER:
-        send(SECOND, ix, ix, dx, 0)
-    for k in range(1, count_x):
-        send(THIRD, ix, ix, k, 0)
+    send(LINE, ix, ix, 3 - 6 * (ix % 2), 0)
 
     all_of(HALO).wait_recv()
 
@@ -494,7 +495,7 @@
         sums[block] = sums[block] + near_sum(target[block], k, columns, False)
         return carry
 
-    lax.fori_loop(0, 32, outer_block, 0, unroll=8)
+    lax.fori_loop(0, 32, outer_block, 0, unroll=16)
 
     @pl.loop(0, 4, unroll=True)
     def _(col):
@@ -591,7 +592,8 @@
         return ok.astype(F32)
 
     for dx in range(-3, 4):
-        line = rows[lax.rem(ix + dx + count_x, count_x)]
+        step = {3: 3 * (1 - ix % 2), -3: -3 * (ix % 2)}.get(dx, dx)
+        line = rows[lax.rem(ix + step + count_x, count_x)]
         line = jnp.concatenate([line, pltpu.roll(line, 127, 1)], 0)
         line = pltpu.roll(line, lax.rem(128 - 16 * iy, 128), 1)
         line = line * within(ix + dx, count_x, dx, ix % 2)

time: 33.8 us -> 32.2 us (0.953)
  Pallas kernels: 32.3 us -> 30.7 us
    pallas_call x1, Pallas kernels: 32.3 us -> 30.7 us  [body(): return call(offsets, charges, *fixed)]
where the time goes in v6:
time: 32.2 us; the launch traced here: 32 us
  Pallas kernels  30.7 us (95%)
  local copies, waits for them, and re-layouts  1.32 us (4%)
    pallas_call x1, Pallas kernels, body(): return call(offsets, charges, *fixed)  30.7 us
    unnamed x1, local copies, waits for them, and re-layouts  1.32 us

profile of v6, /device:TPU:1, one launch (start us, length us, event | category | flops | bytes accessed | tf_op | source)
XLA Modules:
  0.0 32.0 jit_solution(9095516931292405892)
XLA Ops:
  0.0 30.7 %shard_map.46 = f32[2,2,1024]{2,1,0:T(2,128)} custom-call(f32[3,2,2,1024]{3,2,1,0:T(2,128)} %off_hbm.1, f32[2,2,1024]{2,1,0:T(2,128)} %charge_hbm.1, bf16[256,256]{1,0:T(8,128)(2,1)} %constant.4.clone.uf_hbm, bf16[2,512,64]{2,1,0:T(8,128)(2,1)} %constant.5.clone.u2_hbm), custom_call_target="tpu_custom_call" | custom-call | tf_op jit(solution)/shard_map/pallas_call | solution.py:703
  30.7 1.3 %copy.6 = f32[2,2,1024]{2,1,0:T(2,128)} copy(f32[2,2,1024]{2,1,0:T(2,128)} %shard_map.46) | data formatting | bytes 32768

commit v7 on v6

--- a/solution.py
+++ b/solution.py
@@ -13,9 +13,13 @@
 F32 = jnp.float32
 BF16 = jnp.bfloat16
 DIRS = [(ox, oy) for ox in (-1, 0, 1) for oy in (-1, 0, 1) if (ox, oy) != (0, 0)]
-ROWS = (1, 2, -1, -2)
-WIDER = (1, 2, 3, 4, 5, 6, 7, -1, -2, -3, -4, -5, -6, -7)
+ROWS = (2, -2, 1, -1)
+WIDER = (4, -4, 3, -3, 5, -5, 2, -2, 6, -6, 1, -1, 7, -7)
 TILES = 25
+
+
+def hops(k):
+    return min(k % 8, 8 - k % 8) + min(k // 8, 4 - k // 8)
 
 
 def nodes():
@@ -179,7 +183,7 @@
             table3[64 * i : 64 * i + 64, at] = hi
             table3[192 + 64 * i : 256 + 64 * i, at] = lo
 
-    pl.loop(0, 8)(table_tile)
+    pl.loop(0, 9)(table_tile)
 
     def basis(column, k, level=0, col=None):
         places = [halo[column, comp, k : k + 1, :] for comp in range(3)]
@@ -286,7 +290,7 @@
     for ox, oy in DIRS:
         send(LEAF, 4, (1 - ox) * 3 + 1 - oy, ox, oy)
 
-    pl.loop(8, TILES)(table_tile)
+    pl.loop(9, TILES)(table_tile)
 
     @pl.loop(0, 4, unroll=True)
     def _(col):
@@ -467,13 +471,13 @@
         pair = pair + pltpu.roll(packed[2 * e : 2 * e + 2], 16 * e, 1)
     thirds[ix] = pair
 
-    for k in range(1, count_x):
-        send(THIRD, ix, ix, k, 0)
     for dx in WIDER:
         send(SECOND, ix, ix, dx, 0)
+    send(LINE, ix, ix, 3 - 6 * (ix % 2), 0)
     for dx in ROWS:
         send(LINE, ix, ix, dx, 0)
-    send(LINE, ix, ix, 3 - 6 * (ix % 2), 0)
+    for k in sorted(range(1, count_x), key=hops, reverse=True):
+        send(THIRD, ix, ix, k, 0)
 
     all_of(HALO).wait_recv()
 
@@ -591,34 +595,39 @@
             ok = ok & (odd == 1)
         return ok.astype(F32)
 
+    def beside(value, every):
+        high = value.astype(BF16).astype(F32)
+        return jnp.where(lane64 % every == 0, high, pltpu.roll(value - high, 1, 1))
+
+    valid = []
+    for dy in range(-3, 4):
+        one = within(iy + dy, count_y, dy, iy % 2)
+        two = within(iy // 2 + dy, count_y // 2, dy, iy // 2 % 2)
+        valid.append(jnp.where(lane64 < 16, one, jnp.where(lane64 < 32, two, 0.0)))
     for dx in range(-3, 4):
         step = {3: 3 * (1 - ix % 2), -3: -3 * (ix % 2)}.get(dx, dx)
         line = rows[lax.rem(ix + step + count_x, count_x)]
         line = jnp.concatenate([line, pltpu.roll(line, 127, 1)], 0)
+        line = beside(line * within(ix + dx, count_x, dx, ix % 2), 2)
         line = pltpu.roll(line, lax.rem(128 - 16 * iy, 128), 1)
-        line = line * within(ix + dx, count_x, dx, ix % 2)
         x2 = ix // 2 + dx
         base = lax.rem(2 * x2 + 2 * count_x, count_x)
-        pair = seconds[base] + seconds[base + 1]
+        pair = (seconds[base] + seconds[base + 1]) * within(x2, count_x // 2, dx, ix // 2 % 2)
+        pair = [pltpu.roll(pair, (-(g % 4) - 16 * (g // 4)) % 128, 1) if g else pair for g in range(8)]
+        pair = beside(jnp.concatenate(pair, 0), 4)
         pair = pltpu.roll(pair, lax.rem(144 - 32 * (iy // 2), 128), 1)
-        pair = [pltpu.roll(pair, (-(g % 4) - 16 * (g // 4)) % 128, 1) if g else pair for g in range(8)]
-        pair = jnp.concatenate(pair, 0)
-        pair = pair * within(x2, count_x // 2, dx, ix // 2 % 2)
         for dy in range(-3, 4):
-            one = pltpu.roll(line, (-16 * dy) % 128, 1) * within(iy + dy, count_y, dy, iy % 2)
+            one = pltpu.roll(line, (-16 * dy) % 128, 1)
             two = pltpu.roll(pair, (-32 * dy) % 128, 1)
-            two = two * within(iy // 2 + dy, count_y // 2, dy, iy // 2 % 2)
-            value = jnp.where(lane64 < 16, one, two)
-            high = value.astype(BF16).astype(F32)
-            low = jnp.where(lane64 < 64, pltpu.roll(value - high, 32, 1), 0.0)
+            value = jnp.where(lane64 < 16, one, two) * valid[dy + 3]
             at = ((dx + 3) * 7 + dy + 3) * 64
-            right[at : at + 64] = jnp.where(lane64 < 32, high, low).astype(BF16)
+            right[at : at + 64] = value.astype(BF16)
 
     product[...] = dot(table[...], right[...])
 
-    far12 = shifted(0, 96, (1, 2))
+    far12 = shifted(0, 127, (1, 2))
     for i in range(1, 7):
-        far12 = far12 + shifted(i, 96, (1, 2))
+        far12 = far12 + shifted(i, 127, (1, 2))
 
     all_of(THIRD).wait_recv()
     for j in range(count_x // 4):
@@ -626,9 +635,12 @@
         group = jnp.concatenate([group] + [pltpu.roll(group, 128 - 16 * e, 1) for e in range(1, 4)], 0)
         third = [group] + [pltpu.roll(group, 128 - g, 1) for g in range(1, 8)]
         third = jnp.concatenate(third, 0)
-        right3[128 * j : 128 * j + 64] = wide(third)
-        right3[128 * j + 64 : 128 * j + 128] = wide(pltpu.roll(third, 64, 1))
-    o = folded(dot(table3[...], right3[...]), 192)
+        third = beside(third, 8)
+        right3[128 * j : 128 * j + 64] = third.astype(BF16)
+        right3[128 * j + 64 : 128 * j + 128] = pltpu.roll(third, 64, 1).astype(BF16)
+    o = dot(table3[...], right3[...])
+    o = o[:192] + o[192:]
+    o = o + pltpu.roll(o, 127, 1)
     local = o[64:128]
     local = local + jnp.where(lane64 == 0, pltpu.roll(o[128:], 120, 1), 0.0)
     local = local + jnp.where(lane64 == 8, pltpu.roll(o[:64], 8, 1), 0.0)
@@ -685,7 +697,7 @@
             pltpu.VMEM((896, TILES * 128), BF16),
             pltpu.VMEM((384, count_x // 4 * 128), BF16),
             pltpu.VMEM((TILES * 128, 128), BF16),
-            pltpu.VMEM((count_x // 4 * 128, 256), BF16),
+            pltpu.VMEM((count_x // 4 * 128, 128), BF16),
             pltpu.VMEM((896, 128), F32),
             pltpu.VMEM((4, 1024, 128), BF16),
             pltpu.VMEM((64, 128), F32),

time: 32.2 us -> 32.4 us (level)
  no operation moved by 1% of the time
where the time goes in v7:
time: 32.4 us; the launch traced here: 32.2 us
  Pallas kernels  30.9 us (95%)
  local copies, waits for them, and re-layouts  1.32 us (4%)
    pallas_call x1, Pallas kernels, body(): return call(offsets, charges, *fixed)  30.9 us
    unnamed x1, local copies, waits for them, and re-layouts  1.32 us

profile of v7, /device:TPU:1, one launch (start us, length us, event | category | flops | bytes accessed | tf_op | source)
XLA Modules:
  0.0 32.2 jit_solution(499359979405378691)
XLA Ops:
  0.0 30.9 %shard_map.46 = f32[2,2,1024]{2,1,0:T(2,128)} custom-call(f32[3,2,2,1024]{3,2,1,0:T(2,128)} %off_hbm.1, f32[2,2,1024]{2,1,0:T(2,128)} %charge_hbm.1, bf16[256,256]{1,0:T(8,128)(2,1)} %constant.4.clone.uf_hbm, bf16[2,512,64]{2,1,0:T(8,128)(2,1)} %constant.5.clone.u2_hbm), custom_call_target="tpu_custom_call" | custom-call | tf_op jit(solution)/shard_map/pallas_call | solution.py:715
  30.9 1.3 %copy.6 = f32[2,2,1024]{2,1,0:T(2,128)} copy(f32[2,2,1024]{2,1,0:T(2,128)} %shard_map.46) | data formatting | bytes 32768

commit v8 on v4

--- a/solution.py
+++ b/solution.py
@@ -13,9 +13,13 @@
 F32 = jnp.float32
 BF16 = jnp.bfloat16
 DIRS = [(ox, oy) for ox in (-1, 0, 1) for oy in (-1, 0, 1) if (ox, oy) != (0, 0)]
-ROWS = (1, 2, 3, -1, -2, -3)
-WIDER = (1, 2, 3, 4, 5, 6, 7, -1, -2, -3, -4, -5, -6, -7)
+ROWS = (2, -2, 1, -1)
+WIDER = (4, -4, 3, -3, 5, -5, 2, -2, 6, -6, 1, -1, 7, -7)
 TILES = 25
+
+
+def hops(k):
+    return min(k % 8, 8 - k % 8) + min(k // 8, 4 - k // 8)
 
 
 def nodes():
@@ -214,7 +218,7 @@
                 halo[column_of(cx, cy), 3, k : k + 1] = charge_ref[cx, cy : cy + 1, at]
     ROW, HALO, LEAF, LINE, SECOND, THIRD = range(6)
     buffers = (near_rows, halo, moments, rows, seconds, thirds)
-    counts = (count_y - 1, 12, 8, 6, len(WIDER), count_x - 1)
+    counts = (count_y - 1, 12, 8, len(ROWS) + 1, len(WIDER), count_x - 1)
 
     def send(kind, index, at, dx, dy):
         buffer = buffers[kind]
@@ -225,15 +229,6 @@
         part = buffers[kind].at[pl.ds(0, counts[kind])]
         return remote(part, part, send_s.at[kind], recv_s.at[kind], 1, 1)
 
-    pl.semaphore_wait(barrier, len(DIRS) + count_y - 1 + count_x - 1)
-    for ox, oy in DIRS:
-        take_x = {1: [2], -1: [1], 0: [1, 2]}[ox]
-        put_x = {1: [0], -1: [3], 0: [1, 2]}[ox]
-        take_y = {1: (2, 1), -1: (1, 1), 0: (1, 2)}[oy]
-        put_y = {1: 0, -1: 3, 0: 1}[oy]
-        for a, b in zip(take_x, put_x):
-            at = (pl.ds(a * 4 + take_y[0], take_y[1]), pl.ds(b * 4 + put_y, take_y[1]))
-            send(HALO, *at, ox, oy)
     half_row = lax.broadcasted_iota(jnp.int32, (128, 128), 0) // 64
     half_lane = lax.broadcasted_iota(jnp.int32, (128, 128), 1)
     parity = (half_row == half_lane % 2).astype(F32).astype(BF16)
@@ -276,56 +271,21 @@
         packet = packet + pltpu.roll(first[8 * g : 8 * g + 8], 16 * g, 1)
     near_rows[iy] = packet
 
+    pl.semaphore_wait(barrier, len(DIRS) + count_y - 1 + count_x - 1)
     for k in range(1, count_y):
         send(ROW, iy, iy, 0, k)
     for ox, oy in DIRS:
+        take_x = {1: [2], -1: [1], 0: [1, 2]}[ox]
+        put_x = {1: [0], -1: [3], 0: [1, 2]}[ox]
+        take_y = {1: (2, 1), -1: (1, 1), 0: (1, 2)}[oy]
+        put_y = {1: 0, -1: 3, 0: 1}[oy]
+        for a, b in zip(take_x, put_x):
+            at = (pl.ds(a * 4 + take_y[0], take_y[1]), pl.ds(b * 4 + put_y, take_y[1]))
+            send(HALO, *at, ox, oy)
+    for ox, oy in DIRS:
         send(LEAF, 4, (1 - ox) * 3 + 1 - oy, ox, oy)
 
     pl.loop(8, TILES)(table_tile)
-
-    all_of(ROW).wait_recv()
-    packets = [near_rows[k] for k in range(count_y)]
-    full = []
-    for g in range(8):
-        tile = jnp.zeros((8, 128), F32)
-        for k in range(count_y):
-            moved = pltpu.roll(packets[k], 16 * (k - g) % 128, 1) if k != g else packets[k]
-            tile = jnp.where(lane // 16 == k, moved, tile)
-        full.append(tile)
-    full = jnp.concatenate(full, 0)
-    rows[ix] = full[:32] + pltpu.roll(full[32:], 1, 1)
-
-    def part(source, which, step_z, step_y):
-        o = folded(dot(u2_ref[which], wide(source)), 256)
-        return (
-            o[:64]
-            + pltpu.roll(o[64:128], 128 - step_z, 1)
-            + pltpu.roll(o[128:192], 128 - step_y, 1)
-            + pltpu.roll(o[192:], 128 - step_z - step_y, 1)
-        )
-
-    second = part(full, ix % 2, 2, 16)
-    second = jnp.where((lane64 // 16 % 2 == 0) & (lane64 % 4 == 0), second, 0.0)
-    third = part(second, ix // 2 % 2, 4, 32)
-    third = jnp.where((lane64 // 16 % 4 == 0) & (lane64 % 8 == 0), third, 0.0)
-    packed = second[:8]
-    for g in range(1, 8):
-        packed = packed + pltpu.roll(second[8 * g : 8 * g + 8], g % 4 + 16 * (g // 4), 1)
-    seconds[ix] = packed
-    packed = third[:8]
-    for g in range(1, 8):
-        packed = packed + pltpu.roll(third[8 * g : 8 * g + 8], g, 1)
-    pair = packed[:2]
-    for e in range(1, 4):
-        pair = pair + pltpu.roll(packed[2 * e : 2 * e + 2], 16 * e, 1)
-    thirds[ix] = pair
-
-    for dx in ROWS:
-        send(LINE, ix, ix, dx, 0)
-    for dx in WIDER:
-        send(SECOND, ix, ix, dx, 0)
-    for k in range(1, count_x):
-        send(THIRD, ix, ix, k, 0)
 
     first_term = (sub == 0) | (sub == 1) | (sub == 3)
     second_term = (sub == 2) | (sub == 4)
@@ -384,6 +344,51 @@
             stack = jnp.concatenate([upper, lower], 0).T.astype(BF16)
             target[col * 8 + k] = stack[:64]
             target[col * 8 + k + 1] = stack[64:]
+
+    all_of(ROW).wait_recv()
+    packets = [near_rows[k] for k in range(count_y)]
+    full = []
+    for g in range(8):
+        tile = jnp.zeros((8, 128), F32)
+        for k in range(count_y):
+            moved = pltpu.roll(packets[k], 16 * (k - g) % 128, 1) if k != g else packets[k]
+            tile = jnp.where(lane // 16 == k, moved, tile)
+        full.append(tile)
+    full = jnp.concatenate(full, 0)
+    rows[ix] = full[:32] + pltpu.roll(full[32:], 1, 1)
+
+    def part(source, which, step_z, step_y):
+        o = folded(dot(u2_ref[which], wide(source)), 256)
+        return (
+            o[:64]
+            + pltpu.roll(o[64:128], 128 - step_z, 1)
+            + pltpu.roll(o[128:192], 128 - step_y, 1)
+            + pltpu.roll(o[192:], 128 - step_z - step_y, 1)
+        )
+
+    second = part(full, ix % 2, 2, 16)
+    second = jnp.where((lane64 // 16 % 2 == 0) & (lane64 % 4 == 0), second, 0.0)
+    third = part(second, ix // 2 % 2, 4, 32)
+    third = jnp.where((lane64 // 16 % 4 == 0) & (lane64 % 8 == 0), third, 0.0)
+    packed = second[:8]
+    for g in range(1, 8):
+        packed = packed + pltpu.roll(second[8 * g : 8 * g + 8], g % 4 + 16 * (g // 4), 1)
+    seconds[ix] = packed
+    packed = third[:8]
+    for g in range(1, 8):
+        packed = packed + pltpu.roll(third[8 * g : 8 * g + 8], g, 1)
+    pair = packed[:2]
+    for e in range(1, 4):
+        pair = pair + pltpu.roll(packed[2 * e : 2 * e + 2], 16 * e, 1)
+    thirds[ix] = pair
+
+    for dx in WIDER:
+        send(SECOND, ix, ix, dx, 0)
+    send(LINE, ix, ix, 3 - 6 * (ix % 2), 0)
+    for dx in ROWS:
+        send(LINE, ix, ix, dx, 0)
+    for k in sorted(range(1, count_x), key=hops, reverse=True):
+        send(THIRD, ix, ix, k, 0)
 
     all_of(HALO).wait_recv()
 
@@ -457,7 +462,7 @@
         sums[block] = straight + pltpu.roll(crossed, 64, 1)
         return carry
 
-    lax.fori_loop(0, 32, near_block, 0, unroll=8)
+    lax.fori_loop(0, 32, near_block, 0, unroll=16)
 
     @pl.loop(0, 4, unroll=True)
     def _(col):
@@ -468,21 +473,8 @@
             mine = jnp.where(eye, value[64 * k : 64 * k + 64], 0.0)
             near[col, k : k + 1] = jnp.sum(mine, 0, keepdims=True)
 
-    for kind in (LEAF, LINE, SECOND, THIRD):
+    for kind in (LEAF, LINE, SECOND):
         all_of(kind).wait_recv()
-
-    for j in range(count_x // 4):
-        group = thirds[4 * j] + thirds[4 * j + 1] + thirds[4 * j + 2] + thirds[4 * j + 3]
-        group = jnp.concatenate([group] + [pltpu.roll(group, 128 - 16 * e, 1) for e in range(1, 4)], 0)
-        third = [group] + [pltpu.roll(group, 128 - g, 1) for g in range(1, 8)]
-        third = jnp.concatenate(third, 0)
-        right3[128 * j : 128 * j + 64] = wide(third)
-        right3[128 * j + 64 : 128 * j + 128] = wide(pltpu.roll(third, 64, 1))
-    o = folded(dot(table3[...], right3[...]), 192)
-    local = o[64:128]
-    local = local + jnp.where(lane64 == 0, pltpu.roll(o[128:], 120, 1), 0.0)
-    local = local + jnp.where(lane64 == 8, pltpu.roll(o[:64], 8, 1), 0.0)
-    local3 = jnp.where((lane64 < 16) & (lane64 % 8 == 0), 0.125 * local, 0.0)
 
     plain, crossed = {}, {}
     for ox in (-1, 0, 1):
@@ -531,7 +523,8 @@
         return ok.astype(F32)
 
     for dx in range(-3, 4):
-        line = rows[lax.rem(ix + dx + count_x, count_x)]
+        step = {3: 3 * (1 - ix % 2), -3: -3 * (ix % 2)}.get(dx, dx)
+        line = rows[lax.rem(ix + step + count_x, count_x)]
         line = jnp.concatenate([line, pltpu.roll(line, 127, 1)], 0)
         line = pltpu.roll(line, lax.rem(64 - 16 * iy + 128, 128), 1)
         line = line * within(ix + dx, count_x, dx, ix % 2)
@@ -563,6 +556,20 @@
         for level in range(3):
             value = o if dz == 0 else pltpu.roll(o, (-dz * 2**level) % 128, 1)
             far = far + value * flat[at_w + 8 * level + i : at_w + 8 * level + i + 1]
+
+    all_of(THIRD).wait_recv()
+    for j in range(count_x // 4):
+        group = thirds[4 * j] + thirds[4 * j + 1] + thirds[4 * j + 2] + thirds[4 * j + 3]
+        group = jnp.concatenate([group] + [pltpu.roll(group, 128 - 16 * e, 1) for e in range(1, 4)], 0)
+        third = [group] + [pltpu.roll(group, 128 - g, 1) for g in range(1, 8)]
+        third = jnp.concatenate(third, 0)
+        right3[128 * j : 128 * j + 64] = wide(third)
+        right3[128 * j + 64 : 128 * j + 128] = wide(pltpu.roll(third, 64, 1))
+    o = folded(dot(table3[...], right3[...]), 192)
+    local = o[64:128]
+    local = local + jnp.where(lane64 == 0, pltpu.roll(o[128:], 120, 1), 0.0)
+    local = local + jnp.where(lane64 == 8, pltpu.roll(o[:64], 8, 1), 0.0)
+    local3 = jnp.where((lane64 < 16) & (lane64 % 8 == 0), 0.125 * local, 0.0)
 
     def down(source, which, step):
         o = folded(dot(dn_ref[which], wide(source)), 128)

time: 31.9 us -> 30.7 us (0.962)
  Pallas kernels: 30.4 us -> 29.2 us
    pallas_call x1, Pallas kernels: 30.4 us -> 29.2 us  [body(): return call(offsets, charges, *fixed)]
where the time goes in v8:
time: 30.7 us; the launch traced here: 30.6 us
  Pallas kernels  29.2 us (95%)
  local copies, waits for them, and re-layouts  1.32 us (4%)
    pallas_call x1, Pallas kernels, body(): return call(offsets, charges, *fixed)  29.2 us
    unnamed x1, local copies, waits for them, and re-layouts  1.32 us

profile of v8, /device:TPU:1, one launch (start us, length us, event | category | flops | bytes accessed | tf_op | source)
XLA Modules:
  0.0 30.6 jit_solution(5170920455230925145)
XLA Ops:
  0.0 29.2 %shard_map.55 = f32[2,2,1024]{2,1,0:T(2,128)} custom-call(f32[3,2,2,1024]{3,2,1,0:T(2,128)} %off_hbm.1, f32[2,2,1024]{2,1,0:T(2,128)} %charge_hbm.1, bf16[256,256]{1,0:T(8,128)(2,1)} %constant.6.clone.uf_hbm, bf16[2,512,64]{2,1,0:T(8,128)(2,1)} %constant.7.clone.u2_hbm, bf16[4,256,64]{2,1,0:T(8,128)(2,1)} %constant.8.clone.dn_hbm), custom_call_target="tpu_custom_call" | custom-call | tf_op jit(solution)/shard_map/pallas_call | solution.py:661
  29.2 1.3 %copy.7 = f32[2,2,1024]{2,1,0:T(2,128)} copy(f32[2,2,1024]{2,1,0:T(2,128)} %shard_map.55) | data formatting | bytes 32768

commit v9 on v8

--- a/solution.py
+++ b/solution.py
@@ -48,9 +48,7 @@
     uf = np.concatenate(split(uf), 0)
     u2 = up.transpose(0, 1, 2, 4, 3).reshape(2, 256, 64)
     u2 = np.concatenate(split(u2), 1)
-    dn = up.reshape(4, 128, 64)
-    dn = np.concatenate(split(dn), 1)
-    return [uf, u2, dn]
+    return [uf, u2]
 
 
 def pair_split(x):
@@ -73,9 +71,9 @@
 
 def kernel(
     count_x, count_y,
-    off_hbm, charge_hbm, uf_hbm, u2_hbm, dn_hbm,
+    off_hbm, charge_hbm, uf_hbm, u2_hbm,
     out_ref,
-    off_ref, charge_ref, flat, uf_ref, u2_ref, dn_ref,
+    off_ref, charge_ref, flat, uf_ref, u2_ref,
     halo, moments, near_rows, rows, seconds, thirds, pieces, source, charge, target, sums, near,
     table, table3, right, right3, product, bq, leaf, bases,
     load_s, send_s, recv_s,
@@ -84,7 +82,7 @@
         pltpu.make_async_copy(src, dst, load_s.at[i])
         for i, (src, dst) in enumerate(
             [(off_hbm, off_ref), (charge_hbm, charge_ref)]
-            + [(uf_hbm, uf_ref), (u2_hbm, u2_ref), (dn_hbm, dn_ref)]
+            + [(uf_hbm, uf_ref), (u2_hbm, u2_ref)]
         )
     ]
     for load in loads:
@@ -187,10 +185,17 @@
 
     pl.loop(0, 8)(table_tile)
 
-    def basis(column, k):
-        x = 2.0 * halo[column, 0, k : k + 1, :] - 1.0
-        y = 2.0 * halo[column, 1, k : k + 1, :] - 1.0
-        z = 2.0 * halo[column, 2, k : k + 1, :] - 1.0
+    def basis(column, k, level=0, col=None):
+        places = [halo[column, comp, k : k + 1, :] for comp in range(3)]
+        if level:
+            size = 2**level
+            corner = (
+                ((2 * ix + col // 2) % size).astype(F32),
+                ((2 * iy + col % 2) % size).astype(F32),
+                (2 * k) % size + (lane[:1] // 64).astype(F32),
+            )
+            places = [(place + at) * (1.0 / size) for place, at in zip(places, corner)]
+        x, y, z = (2.0 * place - 1.0 for place in places)
 
         def poly(i, u):
             p = [flat[32 * i + 8 * e : 32 * i + 8 * e + 8] for e in range(4)]
@@ -240,7 +245,7 @@
         column = (1 + col // 2) * 4 + 1 + col % 2
         for k in range(8):
             value = basis(column, k)
-            bases[8 * col + k] = value
+            bases[0, 8 * col + k] = value
             value = value * halo[column, 3, k : k + 1, :]
             hi, lo = pair_split(value)
             bq[col, 64 * k : 64 * k + 64] = hi
@@ -286,6 +291,13 @@
         send(LEAF, 4, (1 - ox) * 3 + 1 - oy, ox, oy)
 
     pl.loop(8, TILES)(table_tile)
+
+    @pl.loop(0, 4, unroll=True)
+    def _(col):
+        column = (1 + col // 2) * 4 + 1 + col % 2
+        for level in range(1, 4):
+            for k in range(8):
+                bases[level, 8 * col + k] = basis(column, k, level, col)
 
     first_term = (sub == 0) | (sub == 1) | (sub == 3)
     second_term = (sub == 2) | (sub == 4)
@@ -571,40 +583,23 @@
     local = local + jnp.where(lane64 == 8, pltpu.roll(o[:64], 8, 1), 0.0)
     local3 = jnp.where((lane64 < 16) & (lane64 % 8 == 0), 0.125 * local, 0.0)
 
-    def down(source, which, step):
-        o = folded(dot(dn_ref[which], wide(source)), 128)
-        return jnp.where(lane64 % (2 * step) == 0, o[:64], pltpu.roll(o[64:], step, 1))
-
-    low = lane64 < 16
-    local2 = down(local3, ix // 2 % 2 * 2 + iy // 2 % 2, 4) + pltpu.roll(far, 48, 1)
-    local2 = jnp.where(low & (lane64 % 4 == 0), local2, 0.0)
-    local1 = down(local2, ix % 2 * 2 + iy % 2, 2) + pltpu.roll(far, 64, 1)
-    local1 = jnp.where(low & (lane64 % 2 == 0), local1, 0.0)
-    local0 = far
-    for col in range(4):
-        value = down(local1, col, 1)
-        if col:
-            value = pltpu.roll(value, 16 * col, 1)
-        local0 = local0 + jnp.where(lane64 // 16 == col, value, 0.0)
-    leaf[...] = local0
-
-    @pl.loop(0, 4, unroll=True)
-    def _(col):
-        column = (1 + col // 2) * 4 + 1 + col % 2
-        here = pltpu.roll(leaf[...], lax.rem(128 - 16 * col, 128), 1)
-        for k in range(8):
-            spread = jnp.where(
-                lane64 < 64,
-                jnp.broadcast_to(here[:, 2 * k : 2 * k + 1], (64, 128)),
-                jnp.broadcast_to(here[:, 2 * k + 1 : 2 * k + 2], (64, 128)),
-            )
-            both = bases[8 * col + k] * spread
-            near[col, k : k + 1] = jnp.sum(both, 0, keepdims=True) + near[col, k : k + 1]
-
-    for col in range(4):
-        for k in range(8):
-            at = slice(128 * k, 128 * k + 128)
-            out_ref[col // 2, col % 2 : col % 2 + 1, at] = near[col, k : k + 1]
+    def column(value, at):
+        return jnp.broadcast_to(value[:, at : at + 1], (64, 128))
+
+    for k in range(8):
+        if k % 4 == 0:
+            high3 = column(local3, 2 * k)
+        if k % 2 == 0:
+            high2 = column(far, 80 + 2 * k)
+        high1 = column(far, 64 + 2 * k)
+        for col in range(4):
+            block = 8 * col + k
+            here = 16 * col + 2 * k
+            high0 = jnp.where(lane64 < 64, column(far, here), column(far, here + 1))
+            both = bases[0, block] * high0 + bases[1, block] * high1
+            both = both + bases[2, block] * high2 + bases[3, block] * high3
+            both = jnp.sum(both, 0, keepdims=True) + near[col, k : k + 1]
+            out_ref[col // 2, col % 2 : col % 2 + 1, 128 * k : 128 * k + 128] = both
 
     for kind in range(6):
         all_of(kind).wait_send()
@@ -627,7 +622,6 @@
             pltpu.VMEM((96 + 128 + 56 + 24 + 8, 128), F32),
             pltpu.VMEM(fixed[0].shape, BF16),
             pltpu.VMEM(fixed[1].shape, BF16),
-            pltpu.VMEM(fixed[2].shape, BF16),
             pltpu.VMEM((16, 4, 8, 128), F32),
             pltpu.VMEM((9, 32, 128), F32),
             pltpu.VMEM((count_y, 8, 128), F32),
@@ -647,8 +641,8 @@
             pltpu.VMEM((896, 256), F32),
             pltpu.VMEM((4, 1024, 128), BF16),
             pltpu.VMEM((64, 128), F32),
-            pltpu.VMEM((32, 64, 128), F32),
-            dma((5,)),
+            pltpu.VMEM((4, 32, 64, 128), F32),
+            dma((4,)),
             dma((6,)),
             dma((6,)),
         ],

time: 30.7 us -> 29 us (0.945)
  Pallas kernels: 29.2 us -> 27.5 us
    pallas_call x1, Pallas kernels: 29.2 us -> 27.5 us  [body(): return call(offsets, charges, *fixed)]
where the time goes in v9:
time: 29 us; the launch traced here: 28.8 us
  Pallas kernels  27.5 us (95%)
  local copies, waits for them, and re-layouts  1.32 us (5%)
    pallas_call x1, Pallas kernels, body(): return call(offsets, charges, *fixed)  27.5 us
    unnamed x1, local copies, waits for them, and re-layouts  1.32 us

profile of v9, /device:TPU:1, one launch (start us, length us, event | category | flops | bytes accessed | tf_op | source)
XLA Modules:
  0.0 28.8 jit_solution(6905151875298631365)
XLA Ops:
  0.0 27.5 %shard_map.46 = f32[2,2,1024]{2,1,0:T(2,128)} custom-call(f32[3,2,2,1024]{3,2,1,0:T(2,128)} %off_hbm.1, f32[2,2,1024]{2,1,0:T(2,128)} %charge_hbm.1, bf16[256,256]{1,0:T(8,128)(2,1)} %constant.4.clone.uf_hbm, bf16[2,512,64]{2,1,0:T(8,128)(2,1)} %constant.5.clone.u2_hbm), custom_call_target="tpu_custom_call" | custom-call | tf_op jit(solution)/shard_map/pallas_call | solution.py:655
  27.5 1.3 %copy.6 = f32[2,2,1024]{2,1,0:T(2,128)} copy(f32[2,2,1024]{2,1,0:T(2,128)} %shard_map.46) | data formatting | bytes 32768
